TPU v7x, 128 devices: a whole 4x4x4 slice. The times are simulated.
128 devices in a mesh: seq: 32 (over x, y, z_lo), fsdp: 4 (over z_hi, core).
Axes of the slice: x: 4, y: 4, z: 4 (z_hi: 2, z_lo: 2; z = z_hi * 2 + z_lo), core: 2. Of those that a mesh axis runs over, the one named last changes fastest.
Arguments:
- tokens: bfloat16 [16384, 2048], P(('seq', 'fsdp')), may hold values from -6 to 6
- w_query: bfloat16 [2048, 1024], P('fsdp'), may hold values from -0.125 to 0.125
- w_key: bfloat16 [2048, 1024], P('fsdp'), may hold values from -0.125 to 0.125
- w_value: bfloat16 [2048, 2048], P('fsdp'), may hold values from -0.125 to 0.125
- w_gate_out: bfloat16 [2048, 2048], P('fsdp'), may hold values from -0.125 to 0.125
- w_beta: bfloat16 [2048, 16], P('fsdp'), may hold values from -2 to 2
- w_decay: bfloat16 [2048, 16], P('fsdp'), may hold values from -0.125 to 0.125
- conv_weight: bfloat16 [4, 4096], replicated, may hold values from -3 to 3
- decay_log: float32 [16], replicated, may hold values from -13 to -3
- dt_bias: float32 [16], replicated, may hold values from -1 to 1
- norm_gain: float32 [128], replicated, may hold values from 0.1 to 1.9
- w_out: bfloat16 [2048, 2048], P('fsdp'), may hold values from -0.125 to 0.125
Outputs:
- mixed_out: bfloat16 [16384, 2048], P(('seq', 'fsdp'))
All inputs are finite; a program needn't handle non-finite values.
Results may differ from a plain program's by a relative error of at most 0.018.
Values may be sent and summed in bfloat16 or wider, within the bound.
A program may use at most 128 MiB of HBM per device.

v0:
```python
import jax
import jax.numpy as jnp
from jax import lax
from jax.sharding import PartitionSpec as P

SPAN = 128


def from_behind(value, axis, steps):
    count = lax.axis_size(axis)
    initial, last = (max(0, -steps), min(count, count - steps))
    return lax.ppermute(value, axis, [(source, source + steps) for source in range(initial, last)])


def unit_rows(arrays):
    return arrays * lax.rsqrt(jnp.sum(arrays * arrays, axis=-1, keepdims=True) + 1e-06)


def conv_act(mixed_rows, before_rows, conv_weight):
    extended = jnp.concatenate([before_rows, mixed_rows], axis=0).astype(jnp.float32)
    count_rows = mixed_rows.shape[0]
    taps_count = conv_weight.shape[0]
    summed = conv_weight[0].astype(jnp.float32) * extended[0:count_rows]
    for offset in range(1, taps_count):
        summed = (
            summed
            + conv_weight[offset].astype(jnp.float32) * extended[offset : offset + count_rows]
        )
    return jax.nn.silu(summed).astype(jnp.bfloat16)


def head_inputs(q_cols, k_cols, v_cols, beta_cols, decay_cols, decay_log, dt_bias, head_dim):
    row_count = q_cols.shape[0]
    key_heads = q_cols.shape[1] // head_dim
    value_heads = v_cols.shape[1] // head_dim
    ratio = value_heads // key_heads
    queries = unit_rows(
        q_cols.astype(jnp.float32).reshape(row_count, key_heads, head_dim)
    ) * head_dim ** (-0.5)
    key_rows = unit_rows(k_cols.astype(jnp.float32).reshape(row_count, key_heads, head_dim))
    queries = jnp.repeat(queries, ratio, axis=1)
    key_rows = jnp.repeat(key_rows, ratio, axis=1)
    values = v_cols.astype(jnp.float32).reshape(row_count, value_heads, head_dim)
    beta_gate = jax.nn.sigmoid(beta_cols.astype(jnp.float32))
    log_decay = -jnp.exp(decay_log) * jax.nn.softplus(decay_cols.astype(jnp.float32) + dt_bias)
    return (queries, key_rows, values, beta_gate, log_decay)


def span_terms(queries, key_rows, values, beta_gate, log_decay):
    highest = lax.Precision.HIGHEST
    cumul = jnp.cumsum(log_decay, axis=1)
    size_c = log_decay.shape[1]
    places = jnp.arange(size_c)
    strict = places[:, None] > places[None, :]
    within = places[:, None] >= places[None, :]
    spread = cumul[:, :, None] - cumul[:, None, :]
    fall_strict = jnp.where(strict, jnp.exp(jnp.where(strict, spread, 0.0)), 0.0)
    fall_within = jnp.where(within, jnp.exp(jnp.where(within, spread, 0.0)), 0.0)
    key_key = jnp.einsum("htd,hsd->hts", key_rows, key_rows, precision=highest)
    identity_mat = jnp.eye(size_c, dtype=jnp.float32)
    system = identity_mat + beta_gate[:, :, None] * key_key * fall_strict
    value_dim = values.shape[2]
    right_both = jnp.concatenate(
        [beta_gate[:, :, None] * values, (beta_gate * jnp.exp(cumul))[:, :, None] * key_rows],
        axis=2,
    )
    solved = jax.scipy.linalg.solve_triangular(system, right_both, lower=True)
    pseudo = solved[:, :, :value_dim]
    weights_w = solved[:, :, value_dim:]
    scores = jnp.einsum("htd,hsd->hts", queries, key_rows, precision=highest) * fall_within
    local_out = jnp.einsum("hts,hsv->htv", scores, pseudo, precision=highest)
    query_eff = jnp.exp(cumul)[:, :, None] * queries - jnp.einsum(
        "hts,hsk->htk", scores, weights_w, precision=highest
    )
    tail_fall = jnp.exp(cumul[:, -1:] - cumul)
    eye_key = jnp.eye(key_rows.shape[2], dtype=jnp.float32)
    transfer = jnp.exp(cumul[:, -1])[:, None, None] * eye_key - jnp.einsum(
        "htk,htj->hkj", weights_w * tail_fall[:, :, None], key_rows, precision=highest
    )
    offset_map = jnp.einsum(
        "htv,htk->hvk", pseudo * tail_fall[:, :, None], key_rows, precision=highest
    )
    return (local_out, query_eff, transfer, offset_map)


def gate_norm(core_rows, gate_cols, norm_gain):
    normed = (
        core_rows
        * lax.rsqrt(jnp.mean(core_rows * core_rows, axis=-1, keepdims=True) + 1e-06)
        * norm_gain
    )
    gated = normed * jax.nn.silu(gate_cols.astype(jnp.float32).reshape(core_rows.shape))
    return gated.reshape(core_rows.shape[0], -1).astype(jnp.bfloat16)


def compose(earlier, later):
    highest = lax.Precision.HIGHEST
    joined = jnp.einsum("hik,hkj->hij", earlier[0], later[0], precision=highest)
    shifted = jnp.einsum("hvk,hkj->hvj", earlier[1], later[0], precision=highest) + later[1]
    return (joined, shifted)


def shards(
    tokens,
    w_query,
    w_key,
    w_value,
    w_gate_out,
    w_beta,
    w_decay,
    conv_weight,
    decay_log,
    dt_bias,
    norm_gain,
    w_out,
):
    highest = lax.Precision.HIGHEST
    rim_count = conv_weight.shape[0] - 1
    fsdp_index = lax.axis_index("fsdp")
    head_dim = norm_gain.shape[0]
    key_width = w_query.shape[1]
    pieces = (
        lax.all_gather(w_query, "fsdp", axis=0, tiled=True),
        lax.all_gather(w_key, "fsdp", axis=0, tiled=True),
        lax.all_gather(w_value, "fsdp", axis=0, tiled=True),
        lax.all_gather(w_gate_out, "fsdp", axis=0, tiled=True),
        lax.all_gather(w_beta, "fsdp", axis=0, tiled=True),
        lax.all_gather(w_decay, "fsdp", axis=0, tiled=True),
    )
    sums_all = tuple(
        (jnp.dot(tokens, weight_part, preferred_element_type=jnp.float32) for weight_part in pieces)
    )
    proj_q, proj_k, proj_v, proj_z, proj_b, proj_a = [
        summed.astype(jnp.bfloat16) for summed in sums_all
    ]
    mixed_rows = jnp.concatenate([proj_q, proj_k, proj_v], axis=1)
    before_rows = from_behind(mixed_rows[mixed_rows.shape[0] - rim_count :], ("seq", "fsdp"), 1)
    conv_out = conv_act(mixed_rows, before_rows, conv_weight)
    q_cols, k_cols, v_cols, gate_cols, beta_cols, decay_cols = (
        lax.all_to_all(conv_out[:, :key_width], "fsdp", split_axis=1, concat_axis=0, tiled=True),
        lax.all_to_all(
            conv_out[:, key_width : 2 * key_width], "fsdp", split_axis=1, concat_axis=0, tiled=True
        ),
        lax.all_to_all(
            conv_out[:, 2 * key_width :], "fsdp", split_axis=1, concat_axis=0, tiled=True
        ),
        lax.all_to_all(proj_z, "fsdp", split_axis=1, concat_axis=0, tiled=True),
        lax.all_to_all(proj_b, "fsdp", split_axis=1, concat_axis=0, tiled=True),
        lax.all_to_all(proj_a, "fsdp", split_axis=1, concat_axis=0, tiled=True),
    )
    local_heads = beta_cols.shape[1]
    rates_local = lax.dynamic_slice_in_dim(decay_log, fsdp_index * local_heads, local_heads)
    bias_local = lax.dynamic_slice_in_dim(dt_bias, fsdp_index * local_heads, local_heads)
    queries, key_rows, values, beta_gate, log_decay = head_inputs(
        q_cols, k_cols, v_cols, beta_cols, decay_cols, rates_local, bias_local, head_dim
    )
    row_count = queries.shape[0]
    block_count = row_count // SPAN

    def by_block(arrays):
        return arrays.reshape((block_count, SPAN) + arrays.shape[1:]).swapaxes(1, 2)

    local_out, query_eff, transfer, offset_map = jax.vmap(span_terms)(
        by_block(queries),
        by_block(key_rows),
        by_block(values),
        by_block(beta_gate),
        by_block(log_decay),
    )
    identity_key = jnp.broadcast_to(
        jnp.eye(head_dim, dtype=jnp.float32), (local_heads, head_dim, head_dim)
    )
    zero_state = jnp.zeros((local_heads, head_dim, head_dim), jnp.float32)

    def walk(carried, block_map):
        return (compose(carried, block_map), carried)

    device_map, prefix_maps = lax.scan(walk, (identity_key, zero_state), (transfer, offset_map))

    def relay_turn(turn_index, incoming):
        leaving = (
            jnp.einsum("hvk,hkj->hvj", incoming, device_map[0], precision=highest) + device_map[1]
        )
        return from_behind(leaving.astype(jnp.bfloat16), "seq", 1).astype(leaving.dtype)

    incoming = lax.fori_loop(0, lax.axis_size("seq") - 1, relay_turn, zero_state)
    block_states = (
        jnp.einsum("hvk,nhkj->nhvj", incoming, prefix_maps[0], precision=highest) + prefix_maps[1]
    )
    core = local_out + jnp.einsum("nhtk,nhvk->nhtv", query_eff, block_states, precision=highest)
    core_rows = core.swapaxes(1, 2).reshape(row_count, local_heads, head_dim)
    gated = gate_norm(core_rows, gate_cols, norm_gain)
    return lax.psum_scatter(
        jnp.dot(gated, w_out, preferred_element_type=jnp.float32).astype(jnp.bfloat16),
        "fsdp",
        scatter_dimension=0,
        tiled=True,
    )


def solution(mesh):
    return jax.shard_map(
        shards,
        mesh=mesh,
        in_specs=(
            P(("seq", "fsdp"), None),
            P("fsdp", None),
            P("fsdp", None),
            P("fsdp", None),
            P("fsdp", None),
            P("fsdp", None),
            P("fsdp", None),
            P(),
            P(),
            P(),
            P(),
            P("fsdp", None),
        ),
        out_specs=P(("seq", "fsdp"), None),
        check_vma=False,
    )
```

profile of v0, /device:TPU:21, one launch (start us, length us, event | category | flops | bytes accessed | tf_op | source)
XLA Modules:
  0.0 892.3 jit_solution(4994776825093131565)
XLA Ops:
  9.4 7.6 all_gather.21
  17.9 4.9 all-to-all-start.2
  22.8 7.0 all_gather.22
  32.3 4.8 all-to-all-start.3
  38.6 3.4 all-to-all-done.3
  42.6 8.2 all-gather.7.cloned.1.call-done
  53.7 36.7 %all-gather.5.cloned.1.call-done = bf16[2048,1024]{1,0:T(8,128)(2,1)} async-done(((bf16[512,1024]{1,0:T(8,128)(2,1)}), bf16[2048,1024]{1,0:T(8,128)(2,1)}) %all-gather.5.cloned.1.call-update) | async-done | bytes 4194320 | tf_op jit(solution)/shard_map/all_gather | solution.py:123
  93.2 60.5 %all-gather.9.cloned.1.call-done = bf16[2048,2048]{1,0:T(8,128)(2,1)} async-done(((bf16[512,2048]{1,0:T(8,128)(2,1)}), bf16[2048,2048]{1,0:T(8,128)(2,1)}) %all-gather.9.cloned.1.call-update) | async-done | bytes 8388624 | tf_op jit(solution)/shard_map/all_gather | solution.py:125
  153.7 4.6 convolution_convert_fusion.2
  165.6 7.0 all-to-all-start.1
  172.7 47.1 %all-gather.11.cloned.1.call-done = bf16[2048,2048]{1,0:T(8,128)(2,1)} async-done(((bf16[512,2048]{1,0:T(8,128)(2,1)}), bf16[2048,2048]{1,0:T(8,128)(2,1)}) %all-gather.11.cloned.1.call-update) | async-done | bytes 8388624 | tf_op jit(solution)/shard_map/all_gather | solution.py:126
  219.8 4.6 convolution_convert_fusion.1
  227.4 4.2 all-to-all-start
  234.1 4.3 all-to-all-done
  238.4 5.0 all-to-all-start.4
  249.2 3.4 fusion.27
  252.6 158.6 %custom-call.4 = f32[4,4,1,128,128]{3,4,2,1,0:T(8,128)} custom-call(f32[4,4,1,128,128]{4,3,2,1,0:T(8,128)} %fusion.27), custom_call_target="InvertDiagBlocksLowerTriangular" | custom-call | tf_op jit(solution)/shard_map/vmap(jit(_solve_triangular))/vmap()/triangular_solve | solution.py:67
  413.3 3.3 convolution_multiply_fusion.1
  416.6 4.8 all-to-all-start.5
  435.2 3.1 fusion.40
  438.3 3.2 convolution_subtract_fusion
  441.5 19.5 %while.28 = (s32[]{:T(128)}, f32[4,128,128]{1,2,0:T(8,128)S(1)}, f32[4,128,128]{1,2,0:T(8,128)}, f32[4,4,128,128]{2,3,1,0:T(8,128)}, f32[4,4,128,128]{2,3,1,0:T(...) while((s32[]{:T(128)}, f32[4,128,128]{1,2,0:T(8,128)S(1)}, ...), condition=%wide.region_4.5_spmd.clone, body=%wide.region_3.4_spmd.clone.sunk | while | flops 201523200 | bytes 8128136 | solution.py:178
  462.2 324.6 %while.29 = (s32[]{:T(128)}, f32[4,128,128]{2,1,0:T(8,128)}, f32[4,128,128]{2,1,0:T(8,128)S(1)}, f32[4,128,128]{2,1,0:T(8,128)S(1)}, s32[]{:T(128)}, /*index=5*/s32[]{:T(128)}) while((s32[]{:T(128)}, f32[4,128,128]{2,1,0:T(8,128)}, f32[4,128,128]{2,1,0:T(8,128)S(1)}, f32[4,128,128]{2,1,0:T(8,128)S(1)}, s32[]{:T(128)}, ...), condition=%wide.region_6.7_spmd.clone, body=%wide.region_5.6_spmd.clone.sunk | while | flops 100925440 | bytes 1835127 | solution.py:186
  464.9 5.6 collective-permute-done
  474.5 5.1 collective-permute-done
  483.6 4.7 collective-permute-done
  492.3 4.7 collective-permute-done
  501.0 4.7 collective-permute-done
  509.7 4.7 collective-permute-done
  516.4 4.0 collective-permute-start
  525.1 6.1 collective-permute-start
  535.7 6.3 collective-permute-start
  546.5 6.3 collective-permute-start
  557.3 6.3 collective-permute-start
  568.1 6.5 collective-permute-start
  574.6 3.0 collective-permute-done
  579.7 7.3 collective-permute-start
  587.1 3.1 collective-permute-done
  592.2 5.8 collective-permute-start
  598.1 4.3 collective-permute-done
  604.4 4.0 collective-permute-start
  608.4 3.8 collective-permute-done
  614.3 5.3 collective-permute-start
  619.6 2.9 collective-permute-done
  624.6 5.8 collective-permute-start
  634.8 6.3 collective-permute-start
  645.6 6.3 collective-permute-start
  656.4 6.3 collective-permute-start
  667.2 6.3 collective-permute-start
  678.0 6.3 collective-permute-start
  688.9 6.8 collective-permute-start
  695.7 3.5 collective-permute-done
  701.3 6.5 collective-permute-start
  707.8 3.6 collective-permute-done
  713.6 5.1 collective-permute-start
  718.7 3.5 collective-permute-done
  724.3 5.0 collective-permute-start
  729.3 3.6 collective-permute-done
  735.0 5.4 collective-permute-start
  744.9 6.3 collective-permute-start
  755.7 6.3 collective-permute-start
  766.5 6.3 collective-permute-start
  777.3 6.3 collective-permute-start
  799.0 86.8 %reduce-scatter.2.cloned.1.call-done = bf16[128,2048]{1,0:T(8,128)(2,1)} async-done(((bf16[512,2048]{1,0:T(8,128)(2,1)}), bf16[128,2048]{1,0:T(8,128)(2,1)}) %reduce-scatter.2.cloned.1.call-update) | async-done | bytes 524304 | tf_op jit(solution)/shard_map/reduce_scatter | solution.py:193
  (238 shorter events, 193.8 us)
Async XLA Ops:
  6.5 789.8 %copy-start = (bf16[512,2048]{1,0:T(8,128)(2,1)S(1)}, bf16[512,2048]{1,0:T(8,128)(2,1)}, u32[]{:S(2)}) copy-start(bf16[512,2048]{1,0:T(8,128)(2,1)} %param.27) | copy-start | bytes 6291460
  6.5 44.2 %all-gather.7.cloned.1.call-start = ((), (), s32[]{:S(2)}) async-start(), calls=%async_computation.8 | async-start | bytes 5242880 | tf_op jit(solution)/shard_map/all_gather | solution.py:124
  7.3 83.1 %all-gather.5.cloned.1.call-start = ((), (), s32[]{:S(2)}) async-start(), calls=%async_computation.7 | async-start | bytes 5242880 | tf_op jit(solution)/shard_map/all_gather | solution.py:123
  8.0 9.0 %copy-start.1 = (bf16[128,2048]{1,0:T(8,128)(2,1)S(1)}, bf16[128,2048]{1,0:T(8,128)(2,1)}, u32[]{:S(2)}) copy-start(bf16[128,2048]{1,0:T(8,128)(2,1)} %param.16) | copy-start | bytes 1572868
  8.0 14.8 %copy-start.17 = (bf16[512,16]{0,1:T(8,128)(2,1)S(1)}, bf16[512,16]{0,1:T(8,128)(2,1)}, u32[]{:S(2)}) copy-start(bf16[512,16]{0,1:T(8,128)(2,1)} %param.21) | copy-start | bytes 49156
  8.0 22.5 %copy-start.21 = (f32[128]{0:T(128)S(1)}, f32[128]{0:T(128)}, u32[]{:S(2)}) copy-start(f32[128]{0:T(128)} %param.26) | copy-start | bytes 1540
  8.0 145.7 %all-gather.9.cloned.1.call-start = ((), (), s32[]{:S(2)}) async-start(), calls=%async_computation.9 | async-start | bytes 10485760 | tf_op jit(solution)/shard_map/all_gather | solution.py:125
  8.8 23.2 %copy-start.11 = (bf16[4,4096]{1,0:T(4,128)(2,1)S(1)}, bf16[4,4096]{1,0:T(4,128)(2,1)}, u32[]{:S(2)}) copy-start(bf16[4,4096]{1,0:T(4,128)(2,1)} %param.23) | copy-start | bytes 98308
  8.8 23.2 %copy-start.22 = (f32[16]{0:T(128)S(1)}, f32[16]{0:T(128)}, u32[]{:S(2)}) copy-start(f32[16]{0:T(128)} %param.24) | copy-start | bytes 196
  8.8 23.3 %copy-start.23 = (f32[16]{0:T(128)S(1)}, f32[16]{0:T(128)}, u32[]{:S(2)}) copy-start(f32[16]{0:T(128)} %param.25) | copy-start | bytes 196
  8.8 210.9 %all-gather.11.cloned.1.call-start = ((), (), s32[]{:S(2)}) async-start(), calls=%async_computation.10 | async-start | bytes 10485760 | tf_op jit(solution)/shard_map/all_gather | solution.py:126
  17.9 14.4 %all-to-all-start.2 = ((bf16[128,4,4]{0,2,1:T(4,128)(2,1)}), bf16[128,4,4]{0,2,1:T(4,128)(2,1)S(1)}, u32[]{:S(2)}, u32[]{:S(2)}) async-start(bf16[128,4,4]{0,2,1:T(4,128)(2,1)} %bitcast.10), calls=%async_computation.2 | async-start | bytes 8192 | tf_op jit(solution)/shard_map/all_to_all | solution.py:149
  32.3 9.7 %all-to-all-start.3 = ((bf16[128,4,4]{0,2,1:T(4,128)(2,1)}), bf16[128,4,4]{0,2,1:T(4,128)(2,1)S(1)}, u32[]{:S(2)}, u32[]{:S(2)}) async-start(bf16[128,4,4]{0,2,1:T(4,128)(2,1)} %bitcast.12), calls=%async_computation.3 | async-start | bytes 8192 | tf_op jit(solution)/shard_map/all_to_all | solution.py:148
  158.4 3.9 collective-permute-start.1
  165.6 61.7 %all-to-all-start.1 = ((bf16[128,4,256]{2,0,1:T(8,128)(2,1)}), bf16[128,4,256]{2,0,1:T(8,128)(2,1)S(1)}, u32[]{:S(2)}, u32[]{:S(2)}) async-start(bf16[128,4,256]{2,0,1:T(8,128)(2,1)} %bitcast.144), calls=%async_computation.1 | async-start | bytes 524288 | tf_op jit(solution)/shard_map/all_to_all | solution.py:141
  227.4 11.0 %all-to-all-start = ((bf16[128,4,256]{2,0,1:T(8,128)(2,1)}), bf16[128,4,256]{2,0,1:T(8,128)(2,1)}, u32[]{:S(2)}, u32[]{:S(2)}) async-start(bf16[128,4,256]{2,0,1:T(8,128)(2,1)} %bitcast.145), calls=%async_computation | async-start | bytes 524288 | tf_op jit(solution)/shard_map/all_to_all | solution.py:140
  238.4 178.3 %all-to-all-start.4 = ((bf16[128,4,512]{0,2,1:T(8,128)(2,1)}), bf16[128,4,512]{0,2,1:T(8,128)(2,1)}, u32[]{:S(2)}, u32[]{:S(2)}) async-start(bf16[128,4,512]{0,2,1:T(8,128)(2,1)} %bitcast.16), calls=%async_computation.4 | async-start | bytes 1048576 | tf_op jit(solution)/shard_map/all_to_all | solution.py:144
  244.6 3.2 copy-start.13
  246.7 2.5 copy-start.12
  246.7 2.5 copy-start.15
  246.7 2.5 copy-start.18
  416.6 377.7 %all-to-all-start.5 = ((bf16[128,4,512]{2,0,1:T(8,128)(2,1)}), bf16[128,4,512]{2,0,1:T(8,128)(2,1)}, u32[]{:S(2)}, u32[]{:S(2)}) async-start(bf16[128,4,512]{2,0,1:T(8,128)(2,1)} %bitcast.173), calls=%async_computation.5 | async-start | bytes 1048576 | tf_op jit(solution)/shard_map/all_to_all | solution.py:147
  421.4 464.4 %reduce-scatter.2.cloned.1.call-start = ((), (), s32[]{:S(2)}) async-start(), calls=%async_computation.11 | async-start | bytes 2621440 | tf_op jit(solution)/shard_map/reduce_scatter | solution.py:193
  427.9 2.0 copy-start.3
  430.0 2.9 copy-start.5
  430.0 2.9 copy-start.14
  435.2 3.1 copy-start.20
  441.7 1.9 copy-start.2
  451.3 1.9 copy-start.2
  456.1 1.9 copy-start.2
  462.6 7.9 collective-permute-start
  472.6 7.0 collective-permute-start
  481.7 6.6 collective-permute-start
  490.4 6.6 collective-permute-start
  499.1 6.6 collective-permute-start
  507.7 6.6 collective-permute-start
  516.4 6.6 collective-permute-start
  525.1 8.5 collective-permute-start
  535.7 8.7 collective-permute-start
  546.5 8.7 collective-permute-start
  557.3 8.7 collective-permute-start
  568.1 9.5 %collective-permute-start = (bf16[4,128,128]{2,1,0:T(8,128)(2,1)S(1)}, bf16[4,128,128]{2,1,0:T(8,128)(2,1)S(1)}, u32[]{:S(2)}, u32[]{:S(2)}) collective-permute-start(bf16[4,128,128]{2,1,0:T(8,128)(2,1)S(1)} %fusion.106), channel_id=1, source_target_pairs={{0,4},{4,8},{8,12},{12,16},{16,20},{20,24},{24,28},{28,32},{32,36}... | collective-permute-start | bytes 393224 | tf_op jit(solution)/shard_map/while/body/eval_jaxpr/ppermute | solution.py:12
  579.7 10.4 %collective-permute-start = (bf16[4,128,128]{2,1,0:T(8,128)(2,1)S(1)}, bf16[4,128,128]{2,1,0:T(8,128)(2,1)S(1)}, u32[]{:S(2)}, u32[]{:S(2)}) collective-permute-start(bf16[4,128,128]{2,1,0:T(8,128)(2,1)S(1)} %fusion.106), channel_id=1, source_target_pairs={{0,4},{4,8},{8,12},{12,16},{16,20},{20,24},{24,28},{28,32},{32,36}... | collective-permute-start | bytes 393224 | tf_op jit(solution)/shard_map/while/body/eval_jaxpr/ppermute | solution.py:12
  592.2 10.1 %collective-permute-start = (bf16[4,128,128]{2,1,0:T(8,128)(2,1)S(1)}, bf16[4,128,128]{2,1,0:T(8,128)(2,1)S(1)}, u32[]{:S(2)}, u32[]{:S(2)}) collective-permute-start(bf16[4,128,128]{2,1,0:T(8,128)(2,1)S(1)} %fusion.106), channel_id=1, source_target_pairs={{0,4},{4,8},{8,12},{12,16},{16,20},{20,24},{24,28},{28,32},{32,36}... | collective-permute-start | bytes 393224 | tf_op jit(solution)/shard_map/while/body/eval_jaxpr/ppermute | solution.py:12
  604.4 7.8 collective-permute-start
  614.3 8.2 collective-permute-start
  624.6 8.2 collective-permute-start
  634.8 8.7 collective-permute-start
  645.6 8.7 collective-permute-start
  656.4 8.7 collective-permute-start
  667.2 8.7 collective-permute-start
  678.0 8.8 collective-permute-start
  688.9 10.4 %collective-permute-start = (bf16[4,128,128]{2,1,0:T(8,128)(2,1)S(1)}, bf16[4,128,128]{2,1,0:T(8,128)(2,1)S(1)}, u32[]{:S(2)}, u32[]{:S(2)}) collective-permute-start(bf16[4,128,128]{2,1,0:T(8,128)(2,1)S(1)} %fusion.106), channel_id=1, source_target_pairs={{0,4},{4,8},{8,12},{12,16},{16,20},{20,24},{24,28},{28,32},{32,36}... | collective-permute-start | bytes 393224 | tf_op jit(solution)/shard_map/while/body/eval_jaxpr/ppermute | solution.py:12
  701.3 10.2 %collective-permute-start = (bf16[4,128,128]{2,1,0:T(8,128)(2,1)S(1)}, bf16[4,128,128]{2,1,0:T(8,128)(2,1)S(1)}, u32[]{:S(2)}, u32[]{:S(2)}) collective-permute-start(bf16[4,128,128]{2,1,0:T(8,128)(2,1)S(1)} %fusion.106), channel_id=1, source_target_pairs={{0,4},{4,8},{8,12},{12,16},{16,20},{20,24},{24,28},{28,32},{32,36}... | collective-permute-start | bytes 393224 | tf_op jit(solution)/shard_map/while/body/eval_jaxpr/ppermute | solution.py:12
  713.6 8.6 collective-permute-start
  724.3 8.7 collective-permute-start
  735.0 7.8 collective-permute-start
  744.9 8.7 collective-permute-start
  755.7 8.7 collective-permute-start
  766.5 8.7 collective-permute-start
  777.3 8.7 collective-permute-start
  786.7 2.9 copy-start.8
  786.7 2.9 copy-start.9
  792.5 2.4 copy-start.19
  (7 other events, 10.1 us)
Sparse Core Ops, SparseCore 0:
  9.0 41.6 all-gather.6
  52.4 37.8 all-gather.4
  92.0 61.6 all-gather.8
  155.2 64.4 all-gather.10
  799.1 86.6 reduce-scatter.1
where the time goes:
time: 896 us; the launch traced here: 892 us
  waiting for transfers between devices  349 us (39%)
  other arithmetic  200 us (22%)
  starting transfers between devices  195 us (22%)
  matrix products  97.4 us (11%)
  local copies, waits for them, and re-layouts  22 us (2%)
  blocking collectives  14.7 us (2%)
  between operations  13.6 us (2%)
    ppermute x32, starting transfers between devices, from_behind(): lax.ppermute(value, axis, [(source, source + steps) for source in range(i...  164 us
    another operation x1, other arithmetic, span_terms(): solved = jax.scipy.linalg.solve_triangular(system, right_both, lower=True)  159 us
    ppermute x32, waiting for transfers between devices, from_behind(): lax.ppermute(value, axis, [(source, source + steps) for source in range(i...  99.2 us
    reduce_scatter x1, waiting for transfers between devices, shards(): lax.psum_scatter(jnp.dot(gated, w_out, preferred_element_type=jnp.float32...  86.8 us
    all_gather x1, waiting for transfers between devices, shards(): lax.all_gather(w_value, 'fsdp', axis=0, tiled=True)  60.5 us
    all_gather x1, waiting for transfers between devices, shards(): lax.all_gather(w_gate_out, 'fsdp', axis=0, tiled=True)  47.1 us
    dot_general x31, matrix products, relay_turn(): jnp.einsum('hvk,hkj->hvj', incoming, device_map[0], precision=highest)  40.7 us
    all_gather x1, waiting for transfers between devices, shards(): lax.all_gather(w_query, 'fsdp', axis=0, tiled=True)  36.7 us
  transfers between devices with their start and end apart: 43, of which 38 were waited for; matrix products, arithmetic and copies ran while one was open for 35% of the time, Pallas kernels for 0%

commit v1 on v0

v1 whole, which is shorter than its diff:
```python
import functools

import jax
import jax.numpy as jnp
from jax import lax
from jax.experimental import pallas as pl
from jax.experimental.pallas import tpu as pltpu
from jax.sharding import PartitionSpec as P

MESH = pl.DeviceIdType.MESH
F32 = jnp.float32
BF16 = jnp.bfloat16
ANY = pl.BlockSpec(memory_space=pl.ANY)
VMEM = pl.BlockSpec(memory_space=pltpu.VMEM)
SMEM = pl.BlockSpec(memory_space=pltpu.SMEM)
DMA = pltpu.SemaphoreType.DMA

D = 2048
DSH = 512
TOK = 128
BLK = 512
HALO = 16
ROWS = HALO + BLK
GQ, GV = 256, 512
GC = 2 * GQ + 2 * GV
DH = 128
NH = 4
NCH = BLK // DH
NSEQ = 32


def coords():
    seq, fsdp = lax.axis_index("seq"), lax.axis_index("fsdp")
    return seq, fsdp, seq % 2, fsdp // 2, fsdp % 2


def gather_kernel(
    tok_ref, wq_ref, wk_ref, wv_ref, wz_ref, wba_ref, tok_out, w_out, wba_out, send, recv, loc
):
    seq, fsdp, zlo, zhi, core = coords()
    base = seq - zlo
    sibling = zhi * 2 + 1 - core
    far = (1 - zhi) * 2
    last = fsdp == 3

    near, cross = far + core, far + 1 - core
    weight_peers = [(seq, sibling), (base + 1 - zlo, near), (base + 1 - zlo, cross)]
    token_peers = [(seq, sibling), (seq, near), (seq, cross)]
    signalled = [weight_peers[0]] + weight_peers[1:] + token_peers[1:]

    barrier = pltpu.get_barrier_semaphore()
    for peer in signalled:
        pl.semaphore_signal(barrier, inc=1, device_id=peer, device_id_type=MESH)

    @pl.when(seq > 0)
    def _():
        pl.semaphore_signal(barrier, inc=1, device_id=(seq - 1, 3), device_id_type=MESH)

    sends_halo = jnp.logical_and(last, seq < NSEQ - 1)
    pl.semaphore_wait(barrier, 5 + 4 * sends_halo.astype(jnp.int32))

    def weight_pieces(group):
        q_at = pl.multiple_of(group * GQ, GQ)
        v_at = pl.multiple_of(group * GV, GV)
        return [
            (wq_ref.at[:, pl.ds(q_at, GQ)], w_out.at[fsdp, :, pl.ds(0, GQ)]),
            (wk_ref.at[:, pl.ds(q_at, GQ)], w_out.at[fsdp, :, pl.ds(GQ, GQ)]),
            (wv_ref.at[:, pl.ds(v_at, GV)], w_out.at[fsdp, :, pl.ds(2 * GQ, GV)]),
            (wz_ref.at[:, pl.ds(v_at, GV)], w_out.at[fsdp, :, pl.ds(2 * GQ + GV, GV)]),
            (wba_ref, wba_out.at[fsdp]),
        ]

    started = []
    index = 0
    for peer in token_peers:
        copy = pltpu.make_async_remote_copy(
            tok_ref,
            tok_out.at[pl.ds(pl.multiple_of(HALO + fsdp * TOK, 16), TOK)],
            send.at[index],
            recv.at[index],
            device_id=peer,
            device_id_type=MESH,
        )
        copy.start()
        started.append(copy)
        index += 1
    for peer in weight_peers:
        for source, target in weight_pieces(peer[1]):
            copy = pltpu.make_async_remote_copy(
                source, target, send.at[index], recv.at[index], device_id=peer, device_id_type=MESH
            )
            copy.start()
            started.append(copy)
            index += 1

    def halo_copy(k):
        return pltpu.make_async_remote_copy(
            tok_ref.at[pl.ds(TOK - HALO, HALO)],
            tok_out.at[pl.ds(0, HALO)],
            send.at[index + k],
            recv.at[index],
            device_id=(lax.rem(seq + 1, NSEQ), k),
            device_id_type=MESH,
        )

    @pl.when(sends_halo)
    def _():
        for k in range(4):
            halo_copy(k).start()

    local = [
        (tok_ref, tok_out.at[pl.ds(pl.multiple_of(HALO + fsdp * TOK, 16), TOK)])
    ] + weight_pieces(fsdp)
    copies = []
    for i, (source, target) in enumerate(local):
        copy = pltpu.make_async_copy(source, target, loc.at[i])
        copy.start()
        copies.append(copy)
    for copy in copies:
        copy.wait()
    for copy in started:
        copy.wait()

    @pl.when(sends_halo)
    def _():
        for k in range(4):
            halo_copy(k).wait_send()

    @pl.when(seq > 0)
    def _():
        halo_copy(0).wait_recv()


def gather(tokens, w_query, w_key, w_value, w_gate, wba):
    count = 3 + 15 + 4
    return pl.pallas_call(
        gather_kernel,
        out_shape=(
            jax.ShapeDtypeStruct((ROWS, D), BF16),
            jax.ShapeDtypeStruct((4, DSH, GC), BF16),
            jax.ShapeDtypeStruct((4, 32, DSH), BF16),
        ),
        in_specs=[ANY] * 6,
        out_specs=(ANY, ANY, ANY),
        scratch_shapes=[DMA((count,)), DMA((count,)), DMA((6,))],
        compiler_params=pltpu.CompilerParams(collective_id=0, has_side_effects=True),
        name="gather",
    )(tokens, w_query, w_key, w_value, w_gate, wba)


def nn(a, b):
    return jnp.dot(a.astype(BF16), b.astype(BF16), preferred_element_type=F32)


def nt(a, b):
    return lax.dot_general(
        a.astype(BF16), b.astype(BF16), (((1,), (1,)), ((), ())), preferred_element_type=F32
    )


def tn(a, b):
    return lax.dot_general(
        a.astype(BF16), b.astype(BF16), (((0,), (0,)), ((), ())), preferred_element_type=F32
    )


def full(a, b):
    return jnp.dot(a, b, preferred_element_type=F32, precision=lax.Precision.HIGHEST)


def split(a):
    high = a.astype(BF16)
    return high, (a - high.astype(F32)).astype(BF16)


def fine(a, b):
    ah, al = split(a)
    bh, bl = split(b)
    dot = functools.partial(jnp.dot, preferred_element_type=F32)
    return dot(ah, bh) + dot(al, bh) + dot(ah, bl)


INV = nn


def silu(v):
    return v / (1.0 + jnp.exp(-v))


def local_kernel(
    tok_ref, w_ref, wba_ref, conv_ref, rate_ref, bias_ref,
    core_ref, qt_ref, gate_ref, map_ref,
    mixed, act, small, chain,
):
    seq, fsdp, _, _, _ = coords()

    def project(j):
        total = None
        for part in range(4):
            term = jnp.dot(
                tok_ref[:, pl.ds(part * DSH, DSH)],
                w_ref[part, :, pl.ds(j * 256, 256)],
                preferred_element_type=F32,
            )
            total = term if total is None else total + term
        return total

    for j in range(4):
        mixed[...] = project(j).astype(BF16).astype(F32)

        @pl.when(seq == 0)
        def _():
            mixed[pl.ds(0, HALO), :] = jnp.zeros((HALO, 256), F32)

        if j < 2:
            at = j * 1024 + fsdp * GQ
        else:
            at = 2048 + fsdp * GV + (j - 2) * 256
        taps = conv_ref[:, pl.ds(pl.multiple_of(at, 256), 256)].astype(F32)
        total = taps[0:1, :] * mixed[pl.ds(HALO - 3, BLK), :]
        for i in range(1, 4):
            total = total + taps[i : i + 1, :] * mixed[pl.ds(HALO - 3 + i, BLK), :]
        out = silu(total).astype(BF16).astype(F32)
        for part in range(2):
            head = out[:, part * DH : (part + 1) * DH]
            if j < 2:
                head = head * lax.rsqrt(jnp.sum(head * head, axis=-1, keepdims=True) + 1e-6)
                if j == 0:
                    head = head * DH**-0.5
            act[2 * j + part] = head
    for j in range(2):
        gate_ref[:, pl.ds(j * 256, 256)] = project(4 + j)[HALO:].astype(BF16)

    row = lax.broadcasted_iota(jnp.int32, (8, 32), 0)
    col = lax.broadcasted_iota(jnp.int32, (8, 32), 1)
    pick = (col == jnp.where(row < 4, 0, 12) + fsdp * 4 + row).astype(BF16)
    rows = None
    for part in range(4):
        own = jnp.dot(pick, wba_ref[part], preferred_element_type=F32).astype(BF16)
        term = lax.dot_general(
            own, tok_ref[pl.ds(HALO, BLK), pl.ds(part * DSH, DSH)],
            (((1,), (1,)), ((), ())), preferred_element_type=F32,
        )
        rows = term if rows is None else rows + term
    rows = rows.astype(BF16).astype(F32)
    beta_rows = jax.nn.sigmoid(rows[0:4])
    which = lax.broadcasted_iota(jnp.int32, (4, 1), 0)
    rate = jnp.zeros((4, 1), F32)
    bias = jnp.zeros((4, 1), F32)
    for h in range(4):
        rate = jnp.where(which == h, rate_ref[fsdp * 4 + h], rate)
        bias = jnp.where(which == h, bias_ref[fsdp * 4 + h], bias)
    decay_rows = -jnp.exp(rate) * jax.nn.softplus(rows[4:8] + bias)
    small[...] = jnp.concatenate([decay_rows, beta_rows], axis=0)

    at_row = lax.broadcasted_iota(jnp.int32, (DH, DH), 0)
    at_col = lax.broadcasted_iota(jnp.int32, (DH, DH), 1)
    strict = at_row > at_col
    within = at_row >= at_col
    eye = (at_row == at_col).astype(F32)
    upper = (at_row <= at_col).astype(F32)

    def level(size):
        return jnp.logical_and(
            at_row // (2 * size) == at_col // (2 * size),
            jnp.logical_and(at_row % (2 * size) >= size, at_col % (2 * size) < size),
        )

    base = jnp.logical_and(strict, at_row // 8 == at_col // 8)

    for h in range(NH):
        chain[h, 0:DH] = eye
        chain[h, DH:] = jnp.zeros((DH, DH), F32)

    def chunk(n, carry):
        tokens = pl.ds(pl.multiple_of(n * DH, DH), DH)
        pair = small[:, tokens]
        cumul_rows = full(pair, upper)
        columns = jnp.concatenate([cumul_rows[0:4], pair[4:8]], axis=0).T
        for kh in range(2):
            q = act[kh, tokens, :]
            k = act[2 + kh, tokens, :]
            kk = nt(k, k)
            qk = nt(q, k)
            for h in (2 * kh, 2 * kh + 1):
                v = act[4 + h, tokens, :]
                c = columns[:, h : h + 1]
                b = columns[:, 4 + h : 5 + h]
                last = cumul_rows[h : h + 1, DH - 1 : DH]
                fall = jnp.where(within, jnp.exp(jnp.where(within, c - cumul_rows[h : h + 1, :], 0.0)), 0.0)
                a = jnp.where(strict, b * kk * fall, 0.0)
                scores = qk * fall
                a1 = jnp.where(base, a, 0.0)
                a2 = INV(a1, a1)
                a34 = INV(jnp.concatenate([a1, a2], axis=0), a2)
                x = eye - a1 + a2 - a34[:DH]
                x = x + INV(x, a34[DH:])
                for size in (8, 16, 32, 64):
                    x = x - INV(INV(x, jnp.where(level(size), a, 0.0)), x)
                grow = jnp.exp(c)
                right = jnp.concatenate([b * v, (b * grow) * k], axis=1)
                solved = nn(x, right)
                seen = nn(scores, solved)
                query_eff = grow * q - seen[:, DH:]
                tail = jnp.exp(last - c)
                maps = tn(solved * tail, k)
                transfer = jnp.exp(last) * eye - maps[DH:]
                offset = maps[:DH]
                before = chain[h]
                both = nt(query_eff, before)
                qt_ref[h, tokens, :] = both[:, :DH].astype(BF16)
                core_ref[h, tokens, :] = seen[:, :DH] + both[:, DH:]
                after = nn(before, transfer)
                chain[h, 0:DH] = after[0:DH]
                chain[h, DH:] = after[DH:] + offset
        return carry

    lax.fori_loop(0, NCH, chunk, 0)
    map_ref[...] = chain[...]


def local_terms(tok_all, w_all, wba_all, conv_weight, decay_log, dt_bias):
    return pl.pallas_call(
        local_kernel,
        out_shape=(
            jax.ShapeDtypeStruct((NH, BLK, DH), F32),
            jax.ShapeDtypeStruct((NH, BLK, DH), BF16),
            jax.ShapeDtypeStruct((BLK, GV), BF16),
            jax.ShapeDtypeStruct((NH, 2 * DH, DH), F32),
        ),
        in_specs=[VMEM, VMEM, VMEM, VMEM, SMEM, SMEM],
        out_specs=(VMEM, VMEM, VMEM, VMEM),
        scratch_shapes=[
            pltpu.VMEM((ROWS, 256), F32),
            pltpu.VMEM((8, BLK, DH), F32),
            pltpu.VMEM((8, BLK), F32),
            pltpu.VMEM((NH, 2 * DH, DH), F32),
        ],
        compiler_params=pltpu.CompilerParams(vmem_limit_bytes=48 << 20),
        name="local_terms",
    )(tok_all, w_all, wba_all, conv_weight, decay_log, dt_bias)


ROUNDS = 5


def scan_kernel(map_ref, state_ref, outgoing, arrived, window, before, send, recv):
    seq, fsdp = lax.axis_index("seq"), lax.axis_index("fsdp")
    barrier = pltpu.get_barrier_semaphore()
    for r in range(ROUNDS):
        @pl.when(seq >= 2**r)
        def _():
            pl.semaphore_signal(
                barrier, inc=1, device_id=(seq - 2**r, fsdp), device_id_type=MESH
            )
    targets = sum((seq + 2**r < NSEQ).astype(jnp.int32) for r in range(ROUNDS))

    @pl.when(targets > 0)
    def _():
        pl.semaphore_wait(barrier, targets)

    def copy(r, h):
        return pltpu.make_async_remote_copy(
            outgoing.at[r, h], arrived.at[r, h], send.at[r, h], recv.at[r, h],
            device_id=(lax.rem(seq + 2**r, NSEQ), fsdp), device_id_type=MESH,
        )

    def compose(earlier, later):
        high, low = split(later[0:DH])
        dot = functools.partial(jnp.dot, preferred_element_type=F32)
        out = dot(earlier, high) + dot(earlier, low)
        return out[0:DH], out[DH:] + later[DH:]

    for h in range(NH):
        outgoing[0, h] = map_ref[h].astype(BF16)

        @pl.when(seq + 1 < NSEQ)
        def _():
            copy(0, h).start()

        window[h] = map_ref[h]
        before[h, 0:DH] = jnp.zeros((DH, DH), F32)
        before[h, DH:] = jnp.zeros((DH, DH), F32)

    for r in range(ROUNDS):
        step = 2**r
        for h in range(NH):
            @pl.when(seq >= step)
            def _():
                copy(r, h).wait_recv()
                if r < ROUNDS - 1:
                    top, low = compose(arrived[r, h], window[h])
                    window[h, 0:DH] = top
                    window[h, DH:] = low

            if r < ROUNDS - 1:
                outgoing[r + 1, h] = window[h].astype(BF16)

                @pl.when(seq + 2 * step < NSEQ)
                def _():
                    copy(r + 1, h).start()

            @pl.when(seq >= step)
            def _():
                if r == 0:
                    before[h] = arrived[r, h].astype(F32)
                else:
                    top, low = compose(arrived[r, h], before[h])
                    before[h, 0:DH] = top
                    before[h, DH:] = low

    for h in range(NH):
        state_ref[h] = before[h, DH:]
    for r in range(ROUNDS):
        @pl.when(seq + 2**r < NSEQ)
        def _():
            for h in range(NH):
                copy(r, h).wait_send()


def scan_states(maps):
    return pl.pallas_call(
        scan_kernel,
        out_shape=jax.ShapeDtypeStruct((NH, DH, DH), F32),
        in_specs=[VMEM],
        out_specs=VMEM,
        scratch_shapes=[
            pltpu.VMEM((ROUNDS, NH, 2 * DH, DH), BF16),
            pltpu.VMEM((ROUNDS, NH, 2 * DH, DH), BF16),
            pltpu.VMEM((NH, 2 * DH, DH), F32),
            pltpu.VMEM((NH, 2 * DH, DH), F32),
            DMA((ROUNDS, NH)),
            DMA((ROUNDS, NH)),
        ],
        compiler_params=pltpu.CompilerParams(
            collective_id=1, has_side_effects=True, vmem_limit_bytes=24 << 20
        ),
        name="scan_states",
    )(maps)


def output_kernel(core_ref, qt_ref, gate_ref, state_ref, gain_ref, wout_ref, out_ref, gated):
    gain = gain_ref[...].reshape(1, DH)
    for h in range(NH):
        core = core_ref[h] + nt(qt_ref[h], state_ref[h])
        scale = lax.rsqrt(jnp.mean(core * core, axis=-1, keepdims=True) + 1e-6)
        z = gate_ref[:, pl.ds(h * DH, DH)].astype(F32)
        gated[:, pl.ds(h * DH, DH)] = (core * scale * gain * silu(z)).astype(BF16)
    for j in range(D // 256):
        out_ref[:, pl.ds(j * 256, 256)] = jnp.dot(
            gated[...], wout_ref[:, pl.ds(j * 256, 256)], preferred_element_type=F32
        ).astype(BF16)


def output_terms(core, qt, gate, states, norm_gain, w_out):
    return pl.pallas_call(
        output_kernel,
        out_shape=jax.ShapeDtypeStruct((BLK, D), BF16),
        in_specs=[VMEM] * 6,
        out_specs=VMEM,
        scratch_shapes=[pltpu.VMEM((BLK, GV), BF16)],
        compiler_params=pltpu.CompilerParams(vmem_limit_bytes=40 << 20),
        name="output_terms",
    )(core, qt, gate, states, norm_gain, w_out)


def scatter_kernel(term_ref, out_ref, arrived, send, recv):
    seq, fsdp, _, zhi, core = coords()
    peers = [zhi * 2 + 1 - core, (1 - zhi) * 2 + core, (1 - zhi) * 2 + 1 - core]
    barrier = pltpu.get_barrier_semaphore()
    for peer in peers:
        pl.semaphore_signal(barrier, inc=1, device_id=(seq, peer), device_id_type=MESH)
    pl.semaphore_wait(barrier, 3)
    copies = []
    for i, peer in enumerate(peers):
        copy = pltpu.make_async_remote_copy(
            term_ref.at[pl.ds(pl.multiple_of(peer * TOK, TOK), TOK)],
            arrived.at[i], send.at[i], recv.at[i],
            device_id=(seq, peer), device_id_type=MESH,
        )
        copy.start()
        copies.append(copy)
    for copy in copies:
        copy.wait()
    total = term_ref[pl.ds(pl.multiple_of(fsdp * TOK, TOK), TOK), :].astype(F32)
    for i in range(3):
        total = total + arrived[i].astype(F32)
    out_ref[...] = total.astype(BF16)


def scatter(terms):
    return pl.pallas_call(
        scatter_kernel,
        out_shape=jax.ShapeDtypeStruct((TOK, D), BF16),
        in_specs=[VMEM],
        out_specs=VMEM,
        scratch_shapes=[pltpu.VMEM((3, TOK, D), BF16), DMA((3,)), DMA((3,))],
        compiler_params=pltpu.CompilerParams(
            collective_id=2, has_side_effects=True, vmem_limit_bytes=24 << 20
        ),
        name="scatter",
    )(terms)


def shards(
    tokens, w_query, w_key, w_value, w_gate_out, w_beta, w_decay,
    conv_weight, decay_log, dt_bias, norm_gain, w_out,
):
    wba = jnp.concatenate([w_beta, w_decay], axis=1).T
    tok_all, w_all, wba_all = gather(tokens, w_query, w_key, w_value, w_gate_out, wba)
    core, qt, gate, maps = local_terms(tok_all, w_all, wba_all, conv_weight, decay_log, dt_bias)
    states = scan_states(maps)
    terms = output_terms(core, qt, gate, states, norm_gain, w_out)
    return scatter(terms)


def solution(mesh):
    return jax.shard_map(
        shards,
        mesh=mesh,
        in_specs=(
            P(("seq", "fsdp"), None),
            P("fsdp", None), P("fsdp", None), P("fsdp", None), P("fsdp", None),
            P("fsdp", None), P("fsdp", None),
            P(), P(), P(), P(),
            P("fsdp", None),
        ),
        out_specs=P(("seq", "fsdp"), None),
        check_vma=False,
    )
```

time: 896 us -> 207 us (0.23)
  waiting for transfers between devices: 349 us -> 0 us
  Pallas kernels: 0 us -> 202 us
  other arithmetic: 200 us -> 1.35 us
  starting transfers between devices: 195 us -> 0 us
  matrix products: 97.4 us -> 0 us
  local copies, waits for them, and re-layouts: 22 us -> 3.32 us
  blocking collectives: 14.7 us -> 0 us
  between operations: 13.6 us -> 0.09 us
    pallas_call x0 -> x5, Pallas kernels: none -> 202 us  [the longest x1 99.3 us: gather(): pl.pallas_call(gather_kernel, out_shape=(jax.ShapeDtypeStruct((ROWS, D),...]
    ppermute x32 -> x0, starting transfers between devices: 164 us -> none  [from_behind(): lax.ppermute(value, axis, [(source, source + steps) for source in range(i...]
    another operation x2 -> x0, other arithmetic: 160 us -> none  [the longest x1 159 us: span_terms(): solved = jax.scipy.linalg.solve_triangular(system, right_both, lower=True)]
    all_gather x4 -> x0, waiting for transfers between devices: 152 us -> none  [the longest x1 60.5 us: shards(): lax.all_gather(w_value, 'fsdp', axis=0, tiled=True)]
    ppermute x32 -> x0, waiting for transfers between devices: 99.2 us -> none  [from_behind(): lax.ppermute(value, axis, [(source, source + steps) for source in range(i...]
    dot_general x54 -> x0, matrix products: 95.4 us -> none  [the longest x31 40.7 us: relay_turn(): jnp.einsum('hvk,hkj->hvj', incoming, device_map[0], precision=highest)]
    reduce_scatter x1 -> x0, waiting for transfers between devices: 86.8 us -> none  [shards(): lax.psum_scatter(jnp.dot(gated, w_out, preferred_element_type=jnp.float32...]
    all_to_all x6 -> x0, starting transfers between devices: 30.8 us -> none  [the longest x1 7.02 us: shards(): lax.all_to_all(conv_out[:, key_width:2 * key_width], 'fsdp', split_axis=1...]
  transfers between devices with their start and end apart: 43 -> 0, of which waited for: 38 -> 0; matrix products, arithmetic and copies ran while one was open for 35% -> 0% of each run, Pallas kernels for 0% -> 0%
where the time goes in v1:
time: 207 us; the launch traced here: 206 us
  Pallas kernels  202 us (98%)
  local copies, waits for them, and re-layouts  3.32 us (2%)
    pallas_call x1, Pallas kernels, gather(): pl.pallas_call(gather_kernel, out_shape=(jax.ShapeDtypeStruct((ROWS, D),...  99.3 us
    pallas_call x1, Pallas kernels, local_terms(): pl.pallas_call(local_kernel, out_shape=(jax.ShapeDtypeStruct((NH, BLK, DH...  40.4 us
    pallas_call x1, Pallas kernels, scan_states(): pl.pallas_call(scan_kernel, out_shape=jax.ShapeDtypeStruct((NH, DH, DH),...  31.4 us
    pallas_call x1, Pallas kernels, scatter(): pl.pallas_call(scatter_kernel, out_shape=jax.ShapeDtypeStruct((TOK, D), B...  28.7 us

profile of v1, /device:TPU:21, one launch (start us, length us, event | category | flops | bytes accessed | tf_op | source)
XLA Modules:
  0.0 206.4 jit_solution(5160476796352078842)
XLA Ops:
  0.0 1.4 maximum_bitcast_fusion.wba_ref
  1.4 0.0 copy-start.3
  1.4 0.0 copy-start.4
  1.4 0.0 copy-start.5
  1.4 99.3 %gather.1 = (bf16[528,2048]{1,0:T(8,128)(2,1)}, bf16[4,512,1536]{2,1,0:T(8,128)(2,1)}, bf16[4,32,512]{2,1,0:T(8,128)(2,1)}) custom-call(bf16[128,2048]{1,0:T(8,128)(2,1)} %tok_ref.1, bf16[512,1024]{1,0:T(8,128)(2,1)} %wq_ref.1, bf16[512,1024]{1,0:T(8,128)(2,1)} %wk_ref.1, bf16[512,2048]{1,0:T(8,128)(2,1)} %wv_ref.1, bf16[512,2048]{1,0:T(8,128)(2,1)} %wz_ref.1, ...), custom_call_target="tpu_custom_call" | custom-call | tf_op jit(solution)/shard_map/gather/pallas_call | solution.py:136
  100.6 0.0 copy-done.3
  100.6 0.0 copy-done.4
  100.6 0.0 copy-done.5
  100.7 0.0 copy-start
  100.7 1.6 copy-done
  102.3 0.0 copy-start.2
  102.3 0.9 copy-done.2
  103.2 0.0 copy-start.1
  103.2 0.0 copy-start.6
  103.2 40.4 %local_terms.1 = (f32[4,512,128]{2,1,0:T(8,128)S(1)}, bf16[4,512,128]{2,1,0:T(8,128)(2,1)S(1)}, bf16[512,512]{1,0:T(8,128)(2,1)S(1)}, f32[4,256,128]{2,1,0:T(8,128)S(1)}) custom-call(bf16[528,2048]{1,0:T(8,128)(2,1)S(1)} %copy-done, bf16[4,512,1536]{2,1,0:T(8,128)(2,1)} %get-tuple-element.13.w_ref, bf16[4,32,512]{2,1,0:T(8,128)(2,1)S(1)} %copy-done.2, ...), custom_call_target="tpu_custom_call" | custom-call | tf_op jit(solution)/shard_map/local_terms/pallas_call | solution.py:323
  143.6 31.4 %scan_states.1.state_ref = f32[4,128,128]{2,1,0:T(8,128)S(1)} custom-call(f32[4,256,128]{2,1,0:T(8,128)S(1)} %get-tuple-element.18.map_ref), custom_call_target="tpu_custom_call" | custom-call | tf_op jit(solution)/shard_map/scan_states/pallas_call | solution.py:422
  175.0 0.0 copy-done.1
  175.0 0.0 copy-done.6
  175.1 1.9 output_terms.1.term_ref
  176.9 28.7 %scatter.1 = bf16[128,2048]{1,0:T(8,128)(2,1)S(1)} custom-call(bf16[512,2048]{1,0:T(8,128)(2,1)S(1)} %output_terms.1.term_ref), custom_call_target="tpu_custom_call" | custom-call | tf_op jit(solution)/shard_map/scatter/pallas_call | solution.py:492
  205.6 0.8 copy.14
Async XLA Ops:
  1.4 99.3 %copy-start.3 = (bf16[4,4096]{1,0:T(4,128)(2,1)S(1)}, bf16[4,4096]{1,0:T(4,128)(2,1)}, u32[]{:S(2)}) copy-start(bf16[4,4096]{1,0:T(4,128)(2,1)} %conv_ref.1) | copy-start | bytes 98308
  1.4 99.3 %copy-start.4 = (f32[16]{0:T(128)S(1)}, f32[16]{0:T(128)}, u32[]{:S(2)}) copy-start(f32[16]{0:T(128)} %rate_ref.1) | copy-start | bytes 196
  1.4 99.3 %copy-start.5 = (f32[16]{0:T(128)S(1)}, f32[16]{0:T(128)}, u32[]{:S(2)}) copy-start(f32[16]{0:T(128)} %bias_ref.1) | copy-start | bytes 196
  100.7 1.6 copy-start
  102.3 0.9 copy-start.2
  103.2 71.9 %copy-start.1 = (bf16[512,2048]{1,0:T(8,128)(2,1)S(1)}, bf16[512,2048]{1,0:T(8,128)(2,1)}, u32[]{:S(2)}) copy-start(bf16[512,2048]{1,0:T(8,128)(2,1)} %wout_ref.1) | copy-start | bytes 6291460
  103.2 71.9 %copy-start.6 = (f32[128]{0:T(128)S(1)}, f32[128]{0:T(128)}, u32[]{:S(2)}) copy-start(f32[128]{0:T(128)} %gain_ref.1) | copy-start | bytes 1540

commit v2 on v1

--- a/solution.py
+++ b/solution.py
@@ -34,73 +34,69 @@
     return seq, fsdp, seq % 2, fsdp // 2, fsdp % 2
 
 
+SECTIONS = ((0, GQ), (GQ, GQ), (2 * GQ, GV), (2 * GQ + GV, GV))
+PIECE = DSH // 4
+
+
 def gather_kernel(
-    tok_ref, wq_ref, wk_ref, wv_ref, wz_ref, wba_ref, tok_out, w_out, wba_out, send, recv, loc
+    tok_ref, wq_ref, wk_ref, wv_ref, wz_ref, wba_ref, tok_out, w_out, wba_out,
+    tok_send, tok_recv, ba_send, ba_recv, near_send, near_recv, cut_send, cut_recv,
+    ring_send, ring_recv, loc,
 ):
     seq, fsdp, zlo, zhi, core = coords()
-    base = seq - zlo
-    sibling = zhi * 2 + 1 - core
+    x, y = seq // 8, (seq // 2) % 4
+    sibling = (seq, zhi * 2 + 1 - core)
     far = (1 - zhi) * 2
-    last = fsdp == 3
-
-    near, cross = far + core, far + 1 - core
-    weight_peers = [(seq, sibling), (base + 1 - zlo, near), (base + 1 - zlo, cross)]
-    token_peers = [(seq, sibling), (seq, near), (seq, cross)]
-    signalled = [weight_peers[0]] + weight_peers[1:] + token_peers[1:]
+    across = (seq, far + core)
+    partner = seq - zlo + 1 - zlo
+    partners = [(partner, far + core), (partner, far + 1 - core)]
+    rings = [
+        [(lax.rem(x + d, 4) * 8 + y * 2 + zlo, fsdp) for d in (1, 3, 2)],
+        [(x * 8 + lax.rem(y + d, 4) * 2 + zlo, fsdp) for d in (1, 3, 2)],
+    ]
+    sends_halo = jnp.logical_and(fsdp == 3, seq < NSEQ - 1)
 
     barrier = pltpu.get_barrier_semaphore()
-    for peer in signalled:
+    for peer in [sibling, across] + partners + rings[0] + rings[1]:
         pl.semaphore_signal(barrier, inc=1, device_id=peer, device_id_type=MESH)
 
     @pl.when(seq > 0)
     def _():
         pl.semaphore_signal(barrier, inc=1, device_id=(seq - 1, 3), device_id_type=MESH)
 
-    sends_halo = jnp.logical_and(last, seq < NSEQ - 1)
-    pl.semaphore_wait(barrier, 5 + 4 * sends_halo.astype(jnp.int32))
-
-    def weight_pieces(group):
-        q_at = pl.multiple_of(group * GQ, GQ)
-        v_at = pl.multiple_of(group * GV, GV)
-        return [
-            (wq_ref.at[:, pl.ds(q_at, GQ)], w_out.at[fsdp, :, pl.ds(0, GQ)]),
-            (wk_ref.at[:, pl.ds(q_at, GQ)], w_out.at[fsdp, :, pl.ds(GQ, GQ)]),
-            (wv_ref.at[:, pl.ds(v_at, GV)], w_out.at[fsdp, :, pl.ds(2 * GQ, GV)]),
-            (wz_ref.at[:, pl.ds(v_at, GV)], w_out.at[fsdp, :, pl.ds(2 * GQ + GV, GV)]),
-            (wba_ref, wba_out.at[fsdp]),
-        ]
-
-    started = []
-    index = 0
-    for peer in token_peers:
-        copy = pltpu.make_async_remote_copy(
-            tok_ref,
-            tok_out.at[pl.ds(pl.multiple_of(HALO + fsdp * TOK, 16), TOK)],
-            send.at[index],
-            recv.at[index],
-            device_id=peer,
-            device_id_type=MESH,
-        )
+    pl.semaphore_wait(barrier, 10 + 4 * sends_halo.astype(jnp.int32))
+
+    def remote(source, target, send, recv, peer):
+        return pltpu.make_async_remote_copy(
+            source, target, send, recv, device_id=peer, device_id_type=MESH
+        )
+
+    def token_rows(group):
+        return tok_out.at[pl.ds(pl.multiple_of(HALO + group * TOK, 16), TOK)]
+
+    weights = (wq_ref, wk_ref, wv_ref, wz_ref)
+
+    def columns(section, group):
+        width = SECTIONS[section][1]
+        return pl.ds(pl.multiple_of(group * width, width), width)
+
+    def held(shard, rows, section):
+        start, width = SECTIONS[section]
+        return w_out.at[shard, rows, pl.ds(start, width)]
+
+    all_rows = pl.ds(0, DSH)
+
+    tok_copies = [
+        remote(tok_ref, token_rows(fsdp), tok_send.at[i], tok_recv.at[i], peer)
+        for i, peer in enumerate((across, sibling))
+    ]
+    for copy in tok_copies:
         copy.start()
-        started.append(copy)
-        index += 1
-    for peer in weight_peers:
-        for source, target in weight_pieces(peer[1]):
-            copy = pltpu.make_async_remote_copy(
-                source, target, send.at[index], recv.at[index], device_id=peer, device_id_type=MESH
-            )
-            copy.start()
-            started.append(copy)
-            index += 1
 
     def halo_copy(k):
-        return pltpu.make_async_remote_copy(
-            tok_ref.at[pl.ds(TOK - HALO, HALO)],
-            tok_out.at[pl.ds(0, HALO)],
-            send.at[index + k],
-            recv.at[index],
-            device_id=(lax.rem(seq + 1, NSEQ), k),
-            device_id_type=MESH,
+        return remote(
+            tok_ref.at[pl.ds(TOK - HALO, HALO)], tok_out.at[pl.ds(0, HALO)],
+            tok_send.at[3 + k], tok_recv.at[3], (lax.rem(seq + 1, NSEQ), k),
         )
 
     @pl.when(sends_halo)
@@ -108,18 +104,89 @@
         for k in range(4):
             halo_copy(k).start()
 
-    local = [
-        (tok_ref, tok_out.at[pl.ds(pl.multiple_of(HALO + fsdp * TOK, 16), TOK)])
-    ] + weight_pieces(fsdp)
-    copies = []
-    for i, (source, target) in enumerate(local):
-        copy = pltpu.make_async_copy(source, target, loc.at[i])
+    piece_at = jnp.where(core == 0, x, y)
+    own_piece = pl.ds(pl.multiple_of(piece_at * PIECE, PIECE), PIECE)
+
+    def cut_copy(section, i):
+        peer = partners[i]
+        return remote(
+            weights[section].at[own_piece, columns(section, peer[1])],
+            held(fsdp, own_piece, section),
+            cut_send.at[i, section], cut_recv.at[core, section], peer,
+        )
+
+    for section in range(4):
+        for i in range(2):
+            cut_copy(section, i).start()
+
+    ba_copies = [
+        remote(wba_ref, wba_out.at[fsdp], ba_send.at[i], ba_recv.at[i], peer)
+        for i, peer in enumerate([sibling] + partners)
+    ]
+    for copy in ba_copies:
         copy.start()
-        copies.append(copy)
-    for copy in copies:
+
+    near_copies = [
+        remote(
+            weights[section].at[:, columns(section, sibling[1])],
+            held(fsdp, all_rows, section),
+            near_send.at[section], near_recv.at[section], sibling,
+        )
+        for section in range(4)
+    ]
+    for copy in near_copies:
+        copy.start()
+
+    local = [(tok_ref, token_rows(fsdp)), (wba_ref, wba_out.at[fsdp])] + [
+        (weights[section].at[:, columns(section, fsdp)], held(fsdp, all_rows, section))
+        for section in range(4)
+    ]
+    local_copies = [
+        pltpu.make_async_copy(source, target, loc.at[i])
+        for i, (source, target) in enumerate(local)
+    ]
+    for copy in local_copies:
+        copy.start()
+
+    tok_copies[0].wait_recv()
+    pass_on = remote(
+        token_rows(across[1]), token_rows(across[1]), tok_send.at[2], tok_recv.at[2], sibling
+    )
+    pass_on.start()
+
+    places = [x, y]
+
+    def ring_copy(section, shard, i):
+        rows = pl.ds(pl.multiple_of(places[shard] * PIECE, PIECE), PIECE)
+        block = held(far + shard, rows, section)
+        return remote(
+            block, block, ring_send.at[shard, i, section], ring_recv.at[shard, i, section],
+            rings[shard][i],
+        )
+
+    for section in range(4):
+        for shard in range(2):
+            rows = pl.ds(pl.multiple_of(places[shard] * PIECE, PIECE), PIECE)
+            block = held(far + shard, rows, section)
+            remote(
+                block, block, cut_send.at[0, section], cut_recv.at[shard, section], partners[0]
+            ).wait_recv()
+            for i in range(3):
+                ring_copy(section, shard, i).start()
+
+    for copy in local_copies:
         copy.wait()
-    for copy in started:
+    tok_copies[0].wait_send()
+    tok_copies[1].wait()
+    pass_on.wait()
+    for copy in ba_copies + near_copies:
         copy.wait()
+    for section in range(4):
+        for i in range(2):
+            cut_copy(section, i).wait_send()
+        for shard in range(2):
+            for i in range(3):
+                ring_copy(section, shard, i).wait()
 
     @pl.when(sends_halo)
     def _():
@@ -132,7 +199,6 @@
 
 
 def gather(tokens, w_query, w_key, w_value, w_gate, wba):
-    count = 3 + 15 + 4
     return pl.pallas_call(
         gather_kernel,
         out_shape=(
@@ -142,7 +208,10 @@
         ),
         in_specs=[ANY] * 6,
         out_specs=(ANY, ANY, ANY),
-        scratch_shapes=[DMA((count,)), DMA((count,)), DMA((6,))],
+        scratch_shapes=[
+            DMA((7,)), DMA((4,)), DMA((3,)), DMA((3,)), DMA((4,)), DMA((4,)),
+            DMA((2, 4)), DMA((2, 4)), DMA((2, 3, 4)), DMA((2, 3, 4)), DMA((6,)),
+        ],
         compiler_params=pltpu.CompilerParams(collective_id=0, has_side_effects=True),
         name="gather",
     )(tokens, w_query, w_key, w_value, w_gate, wba)

time: 207 us -> 179 us (0.86)
  Pallas kernels: 202 us -> 174 us
    pallas_call x1, Pallas kernels: 99.3 us -> 71 us  [gather(): pl.pallas_call(gather_kernel, out_shape=(jax.ShapeDtypeStruct((ROWS, D),...]
where the time goes in v2:
time: 179 us
  Pallas kernels  174 us (97%)
  local copies, waits for them, and re-layouts  3.32 us (2%)
    pallas_call x1, Pallas kernels, gather(): pl.pallas_call(gather_kernel, out_shape=(jax.ShapeDtypeStruct((ROWS, D),...  71 us
    pallas_call x1, Pallas kernels, local_terms(): pl.pallas_call(local_kernel, out_shape=(jax.ShapeDtypeStruct((NH, BLK, DH...  40.4 us
    pallas_call x1, Pallas kernels, scan_states(): pl.pallas_call(scan_kernel, out_shape=jax.ShapeDtypeStruct((NH, DH, DH),...  31.6 us
    pallas_call x1, Pallas kernels, scatter(): pl.pallas_call(scatter_kernel, out_shape=jax.ShapeDtypeStruct((TOK, D), B...  29.1 us

profile of v2, /device:TPU:21, one launch (start us, length us, event | category | flops | bytes accessed | tf_op | source)
XLA Modules:
  0.0 178.7 jit_solution(5663743472528938610)
XLA Ops:
  0.0 1.4 maximum_bitcast_fusion.wba_ref
  1.4 0.0 copy-start.3
  1.4 0.0 copy-start.4
  1.4 0.0 copy-start.5
  1.4 71.0 %gather.1 = (bf16[528,2048]{1,0:T(8,128)(2,1)}, bf16[4,512,1536]{2,1,0:T(8,128)(2,1)}, bf16[4,32,512]{2,1,0:T(8,128)(2,1)}) custom-call(bf16[128,2048]{1,0:T(8,128)(2,1)} %tok_ref.1, bf16[512,1024]{1,0:T(8,128)(2,1)} %wq_ref.1, bf16[512,1024]{1,0:T(8,128)(2,1)} %wk_ref.1, bf16[512,2048]{1,0:T(8,128)(2,1)} %wv_ref.1, bf16[512,2048]{1,0:T(8,128)(2,1)} %wz_ref.1, ...), custom_call_target="tpu_custom_call" | custom-call | tf_op jit(solution)/shard_map/gather/pallas_call | solution.py:202
  72.3 0.0 copy-done.3
  72.3 0.0 copy-done.4
  72.3 0.0 copy-done.5
  72.4 0.0 copy-start
  72.4 1.6 copy-done
  74.0 0.0 copy-start.2
  74.0 0.9 copy-done.2
  74.9 0.0 copy-start.1
  74.9 0.0 copy-start.6
  74.9 40.4 %local_terms.1 = (f32[4,512,128]{2,1,0:T(8,128)S(1)}, bf16[4,512,128]{2,1,0:T(8,128)(2,1)S(1)}, bf16[512,512]{1,0:T(8,128)(2,1)S(1)}, f32[4,256,128]{2,1,0:T(8,128)S(1)}) custom-call(bf16[528,2048]{1,0:T(8,128)(2,1)S(1)} %copy-done, bf16[4,512,1536]{2,1,0:T(8,128)(2,1)} %get-tuple-element.13.w_ref, bf16[4,32,512]{2,1,0:T(8,128)(2,1)S(1)} %copy-done.2, ...), custom_call_target="tpu_custom_call" | custom-call | tf_op jit(solution)/shard_map/local_terms/pallas_call | solution.py:392
  115.3 31.6 %scan_states.1.state_ref = f32[4,128,128]{2,1,0:T(8,128)S(1)} custom-call(f32[4,256,128]{2,1,0:T(8,128)S(1)} %get-tuple-element.18.map_ref), custom_call_target="tpu_custom_call" | custom-call | tf_op jit(solution)/shard_map/scan_states/pallas_call | solution.py:491
  146.9 0.0 copy-done.1
  146.9 0.0 copy-done.6
  146.9 1.9 %output_terms.1.term_ref = bf16[512,2048]{1,0:T(8,128)(2,1)S(1)} custom-call(f32[4,512,128]{2,1,0:T(8,128)S(1)} %get-tuple-element.15.core_ref, bf16[4,512,128]{2,1,0:T(8,128)(2,1)S(1)} %get-tuple-element.16.qt_ref, bf16[512,512]{1,0:T(8,128)(2,1)S(1)} %get-tuple-element.17.gate_ref, f32[4,128,128]{2,1,0:T(8,128)S(1)} %scan_states.1.state_ref, ...), custom_call_target="tpu_custom_call" | custom-call | tf_op jit(solution)/shard_map/output_terms/pallas_call | solution.py:525
  148.7 29.1 %scatter.1 = bf16[128,2048]{1,0:T(8,128)(2,1)S(1)} custom-call(bf16[512,2048]{1,0:T(8,128)(2,1)S(1)} %output_terms.1.term_ref), custom_call_target="tpu_custom_call" | custom-call | tf_op jit(solution)/shard_map/scatter/pallas_call | solution.py:561
  177.9 0.8 copy.14
Async XLA Ops:
  1.4 71.0 %copy-start.3 = (bf16[4,4096]{1,0:T(4,128)(2,1)S(1)}, bf16[4,4096]{1,0:T(4,128)(2,1)}, u32[]{:S(2)}) copy-start(bf16[4,4096]{1,0:T(4,128)(2,1)} %conv_ref.1) | copy-start | bytes 98308
  1.4 71.0 %copy-start.4 = (f32[16]{0:T(128)S(1)}, f32[16]{0:T(128)}, u32[]{:S(2)}) copy-start(f32[16]{0:T(128)} %rate_ref.1) | copy-start | bytes 196
  1.4 71.0 %copy-start.5 = (f32[16]{0:T(128)S(1)}, f32[16]{0:T(128)}, u32[]{:S(2)}) copy-start(f32[16]{0:T(128)} %bias_ref.1) | copy-start | bytes 196
  72.4 1.6 copy-start
  74.0 0.9 copy-start.2
  74.9 72.0 %copy-start.1 = (bf16[512,2048]{1,0:T(8,128)(2,1)S(1)}, bf16[512,2048]{1,0:T(8,128)(2,1)}, u32[]{:S(2)}) copy-start(bf16[512,2048]{1,0:T(8,128)(2,1)} %wout_ref.1) | copy-start | bytes 6291460
  74.9 72.0 %copy-start.6 = (f32[128]{0:T(128)S(1)}, f32[128]{0:T(128)}, u32[]{:S(2)}) copy-start(f32[128]{0:T(128)} %gain_ref.1) | copy-start | bytes 1540

commit v3 on v2

v3 whole, which is shorter than its diff:
```python
import functools

import jax
import jax.numpy as jnp
from jax import lax
from jax.experimental import pallas as pl
from jax.experimental.pallas import tpu as pltpu
from jax.sharding import PartitionSpec as P

MESH = pl.DeviceIdType.MESH
F32 = jnp.float32
BF16 = jnp.bfloat16
HBM = pl.BlockSpec(memory_space=pltpu.HBM)
VMEM = pl.BlockSpec(memory_space=pltpu.VMEM)
SMEM = pl.BlockSpec(memory_space=pltpu.SMEM)
DMA = pltpu.SemaphoreType.DMA

D = 2048
DSH = 512
TOK = 128
BLK = 512
HALO = 16
ROWS = HALO + BLK
GQ, GV = 256, 512
GC = 2 * GQ + 2 * GV
DH = 128
NH = 4
NCH = BLK // DH
NSEQ = 32
ROUNDS = 5


def coords():
    seq, fsdp = lax.axis_index("seq"), lax.axis_index("fsdp")
    return seq, fsdp, seq % 2, fsdp // 2, fsdp % 2


def nn(a, b):
    return jnp.dot(a.astype(BF16), b.astype(BF16), preferred_element_type=F32)


def full(a, b):
    return jnp.dot(a, b, preferred_element_type=F32, precision=lax.Precision.HIGHEST)


def split(a):
    high = a.astype(BF16)
    return high, (a - high.astype(F32)).astype(BF16)


def silu(v):
    return v / (1.0 + jnp.exp(-v))


SECTIONS = ((0, GQ), (GQ, GQ), (2 * GQ, GV), (2 * GQ + GV, GV))
PIECE = DSH // 4
UNITS = NCH * NH
TOGETHER = 8


def layer_kernel(
    tok_ref, wq_ref, wk_ref, wv_ref, wz_ref, wba_ref, wo_ref, conv_ref, rate_ref, bias_ref, gain_ref,
    out_ref,
    tok_all, w_all, wba_all, mixed, act, small, cols, key_t, system, scores,
    core_ref, qt_ref, gate_ref, wo_all, outgoing, arrived, window, before, gated, gated_all, total_ref,
    tok_send, tok_recv, ba_send, ba_recv, near_send, near_recv, cut_send, cut_recv,
    ring_send, ring_recv, loc, wo_send, wo_recv, scan_send, scan_recv, gate_send, gate_recv,
):
    seq, fsdp, zlo, zhi, core = coords()
    x, y = seq // 8, (seq // 2) % 4
    sibling = (seq, zhi * 2 + 1 - core)
    far = (1 - zhi) * 2
    across = (seq, far + core)
    cross = (seq, far + 1 - core)
    partner = seq - zlo + 1 - zlo
    partners = [(partner, far + core), (partner, far + 1 - core)]
    rings = [
        [(lax.rem(x + d, 4) * 8 + y * 2 + zlo, fsdp) for d in (1, 3, 2)],
        [(x * 8 + lax.rem(y + d, 4) * 2 + zlo, fsdp) for d in (1, 3, 2)],
    ]
    sends_halo = jnp.logical_and(fsdp == 3, seq < NSEQ - 1)

    barrier = pltpu.get_barrier_semaphore()
    for peer in [sibling, across, cross] + partners + rings[0] + rings[1]:
        pl.semaphore_signal(barrier, inc=1, device_id=peer, device_id_type=MESH)
    for r in range(ROUNDS):
        @pl.when(seq >= 2**r)
        def _():
            pl.semaphore_signal(
                barrier, inc=1, device_id=(seq - 2**r, fsdp), device_id_type=MESH
            )

    @pl.when(seq > 0)
    def _():
        pl.semaphore_signal(barrier, inc=1, device_id=(seq - 1, 3), device_id_type=MESH)

    def remote(source, target, send, recv, peer):
        return pltpu.make_async_remote_copy(
            source, target, send, recv, device_id=peer, device_id_type=MESH
        )

    def token_rows(group):
        return tok_all.at[pl.ds(pl.multiple_of(HALO + group * TOK, 16), TOK)]

    weights = (wq_ref, wk_ref, wv_ref, wz_ref)

    def columns(section, group):
        width = SECTIONS[section][1]
        return pl.ds(pl.multiple_of(group * width, width), width)

    def held(shard, rows, section):
        start, width = SECTIONS[section]
        return w_all.at[shard, rows, pl.ds(start, width)]

    all_rows = pl.ds(0, DSH)
    local = [(tok_ref, token_rows(fsdp)), (wba_ref, wba_all.at[fsdp])] + [
        (weights[section].at[:, columns(section, fsdp)], held(fsdp, all_rows, section))
        for section in range(4)
    ] + [(wo_ref, wo_all.at[fsdp])]
    local_copies = [
        pltpu.make_async_copy(source, target, loc.at[i])
        for i, (source, target) in enumerate(local)
    ]
    for copy in local_copies:
        copy.start()

    onward = sum((seq + 2**r < NSEQ).astype(jnp.int32) for r in range(ROUNDS))
    pl.semaphore_wait(barrier, 11 + 4 * sends_halo.astype(jnp.int32) + onward)

    tok_copies = [
        remote(tok_ref, token_rows(fsdp), tok_send.at[i], tok_recv.at[i], peer)
        for i, peer in enumerate((across, sibling))
    ]
    for copy in tok_copies:
        copy.start()

    piece_at = jnp.where(core == 0, x, y)
    own_piece = pl.ds(pl.multiple_of(piece_at * PIECE, PIECE), PIECE)

    def cut_copy(section, i):
        peer = partners[i]
        return remote(
            weights[section].at[own_piece, columns(section, peer[1])],
            held(fsdp, own_piece, section),
            cut_send.at[i, section], cut_recv.at[core, section], peer,
        )

    for section in range(4):
        for i in range(2):
            cut_copy(section, i).start()

    def halo_copy(k):
        return remote(
            tok_ref.at[pl.ds(TOK - HALO, HALO)], tok_all.at[pl.ds(0, HALO)],
            tok_send.at[3 + k], tok_recv.at[3], (lax.rem(seq + 1, NSEQ), k),
        )

    @pl.when(sends_halo)
    def _():
        for k in range(4):
            halo_copy(k).start()

    ba_copies = [
        remote(wba_ref, wba_all.at[fsdp], ba_send.at[i], ba_recv.at[i], peer)
        for i, peer in enumerate([sibling] + partners)
    ]
    for copy in ba_copies:
        copy.start()

    near_copies = [
        remote(
            weights[section].at[:, columns(section, sibling[1])],
            held(fsdp, all_rows, section),
            near_send.at[section], near_recv.at[section], sibling,
        )
        for section in range(4)
    ]
    for copy in near_copies:
        copy.start()

    places = [x, y]

    def ring_copy(section, shard, i):
        rows = pl.ds(pl.multiple_of(places[shard] * PIECE, PIECE), PIECE)
        block = held(far + shard, rows, section)
        return remote(
            block, block, ring_send.at[shard, i, section], ring_recv.at[shard, i, section],
            rings[shard][i],
        )

    def pass_round(section):
        for shard in range(2):
            rows = pl.ds(pl.multiple_of(places[shard] * PIECE, PIECE), PIECE)
            block = held(far + shard, rows, section)
            remote(
                block, block, cut_send.at[0, section], cut_recv.at[shard, section], partners[0]
            ).wait_recv()
            for i in range(3):
                ring_copy(section, shard, i).start()

    wo_at = pl.ds(pl.multiple_of(piece_at * PIECE, PIECE), PIECE)
    wo_ring = [
        (jnp.where(core == 0, rings[0][i][0], rings[1][i][0]), fsdp) for i in range(3)
    ]

    def wo_beside():
        return remote(wo_ref, wo_all.at[fsdp], wo_send.at[0], wo_recv.at[0], sibling)

    def wo_cut():
        return remote(
            wo_ref.at[wo_at], wo_all.at[fsdp, wo_at], wo_send.at[1], wo_recv.at[1], partners[0]
        )

    def wo_round(i):
        block = wo_all.at[far + core, wo_at]
        return remote(block, block, wo_send.at[2 + i], wo_recv.at[2 + i], wo_ring[i])

    def wo_share():
        block = wo_all.at[far + core]
        return remote(block, block, wo_send.at[5], wo_recv.at[5], sibling)

    def arrive(section):
        local_copies[2 + section].wait()
        near_copies[section].wait_recv()
        for shard in range(2):
            for i in range(3):
                ring_copy(section, shard, i).wait_recv()

    def project(j):
        total = None
        for part in range(4):
            term = jnp.dot(
                tok_all[:, pl.ds(part * DSH, DSH)],
                w_all[part, :, pl.ds(j * 256, 256)],
                preferred_element_type=F32,
            )
            total = term if total is None else total + term
        return total

    def convolve(j):
        mixed[...] = project(j).astype(BF16).astype(F32)

        @pl.when(seq == 0)
        def _():
            mixed[pl.ds(0, HALO), :] = jnp.zeros((HALO, 256), F32)

        if j < 2:
            at = j * 1024 + fsdp * GQ
        else:
            at = 2048 + fsdp * GV + (j - 2) * 256
        taps = conv_ref[:, pl.ds(pl.multiple_of(at, 256), 256)].astype(F32)
        total = taps[0:1, :] * mixed[pl.ds(HALO - 3, BLK), :]
        for i in range(1, 4):
            total = total + taps[i : i + 1, :] * mixed[pl.ds(HALO - 3 + i, BLK), :]
        out = silu(total).astype(BF16).astype(F32)
        for part in range(2):
            head = out[:, part * DH : (part + 1) * DH]
            if j < 2:
                head = head * lax.rsqrt(jnp.sum(head * head, axis=-1, keepdims=True) + 1e-6)
                if j == 0:
                    head = head * DH**-0.5
            act[2 * j + part] = head

    at_row = lax.broadcasted_iota(jnp.int32, (DH, DH), 0)
    at_col = lax.broadcasted_iota(jnp.int32, (DH, DH), 1)
    strict = at_row > at_col
    within = at_row >= at_col
    eye = (at_row == at_col).astype(F32)
    upper = (at_row <= at_col).astype(F32)

    pass_round(0)
    tok_copies[0].wait_recv()
    pass_on = remote(
        token_rows(across[1]), token_rows(across[1]), tok_send.at[2], tok_recv.at[2], sibling
    )
    pass_on.start()
    pass_round(1)

    local_copies[0].wait()
    local_copies[1].wait()
    tok_copies[1].wait_recv()
    pass_on.wait_recv()
    for copy in ba_copies:
        copy.wait_recv()

    @pl.when(seq > 0)
    def _():
        halo_copy(0).wait_recv()

    row = lax.broadcasted_iota(jnp.int32, (8, 32), 0)
    col = lax.broadcasted_iota(jnp.int32, (8, 32), 1)
    pick = (col == jnp.where(row < 4, 0, 12) + fsdp * 4 + row).astype(BF16)
    rows = None
    for part in range(4):
        own = jnp.dot(pick, wba_all[part], preferred_element_type=F32).astype(BF16)
        term = lax.dot_general(
            own, tok_all[pl.ds(HALO, BLK), pl.ds(part * DSH, DSH)],
            (((1,), (1,)), ((), ())), preferred_element_type=F32,
        )
        rows = term if rows is None else rows + term
    rows = rows.astype(BF16).astype(F32)
    beta_rows = jax.nn.sigmoid(rows[0:4])
    which = lax.broadcasted_iota(jnp.int32, (4, 1), 0)
    rate = jnp.zeros((4, 1), F32)
    bias = jnp.zeros((4, 1), F32)
    for h in range(4):
        rate = jnp.where(which == h, rate_ref[fsdp * 4 + h], rate)
        bias = jnp.where(which == h, bias_ref[fsdp * 4 + h], bias)
    decay_rows = -jnp.exp(rate) * jax.nn.softplus(rows[4:8] + bias)
    for n in range(NCH):
        at = slice(n * DH, (n + 1) * DH)
        pair = jnp.concatenate([decay_rows[:, at], beta_rows[:, at]], axis=0)
        cumul = full(pair, upper)
        small[n] = cumul
        cols[n] = jnp.concatenate([cumul[0:4], pair[4:8]], axis=0).T

    arrive(0)
    convolve(0)
    pass_round(2)
    arrive(1)
    convolve(1)
    pass_round(3)

    def fall_of(n, h):
        gap = cols[n][:, h : h + 1] - small[n][h : h + 1, :]
        return jnp.where(within, jnp.exp(jnp.where(within, gap, 0.0)), 0.0)

    def pairs(n, carry):
        tokens = pl.ds(pl.multiple_of(n * DH, DH), DH)
        for kh in range(2):
            q = act[kh, tokens, :]
            k = act[2 + kh, tokens, :]
            kt = k.T.astype(BF16)
            key_t[n * 2 + kh] = kt
            both = nn(jnp.concatenate([k, q], axis=0), kt)
            for h in (2 * kh, 2 * kh + 1):
                fall = fall_of(n, h)
                b = cols[n][:, 4 + h : 5 + h]
                system[n * NH + h] = jnp.where(strict, b * both[:DH] * fall, 0.0).astype(BF16)
                scores[n * NH + h] = (both[DH:] * fall).astype(BF16)
        return carry

    lax.fori_loop(0, NCH, pairs, 0)

    def same(size):
        return at_row // size == at_col // size

    mask8 = jnp.logical_and(strict, same(8)).astype(BF16)
    mask32 = jnp.logical_and(strict, jnp.logical_and(same(32), jnp.logical_not(same(8)))).astype(BF16)
    mask128 = jnp.logical_and(strict, jnp.logical_not(same(32))).astype(BF16)

    def invert(g, carry):
        ids = [g * TOGETHER + i for i in range(TOGETHER)]
        every = range(TOGETHER)
        a1 = [system[u] * mask8 for u in ids]
        a2 = [nn(a, a) for a in a1]
        a34 = [nn(jnp.concatenate([a1[i], a2[i].astype(BF16)], axis=0), a2[i]) for i in every]
        xs = [eye - a1[i].astype(F32) + a2[i] - a34[i][:DH] for i in every]
        xs = [(xs[i] + nn(xs[i], a34[i][DH:])).astype(BF16) for i in every]
        for mask in (mask32, mask128):
            ys = [nn(xs[i], system[ids[i]] * mask).astype(BF16) for i in every]
            yx = [nn(ys[i], jnp.concatenate([ys[i], xs[i]], axis=1)) for i in every]
            zs = [(xs[i].astype(F32) - yx[i][:, DH:]).astype(BF16) for i in every]
            xs = [(zs[i].astype(F32) + nn(yx[i][:, :DH], zs[i])).astype(BF16) for i in every]
        for i in every:
            system[ids[i]] = xs[i]
        return carry

    lax.fori_loop(0, UNITS // TOGETHER, invert, 0)

    arrive(2)
    wo_beside().start()
    wo_cut().start()
    convolve(2)
    convolve(3)

    def scan_copy(r, h):
        cut = pl.ds(0, 2 * DH) if r < ROUNDS - 1 else pl.ds(DH, DH)
        return remote(
            outgoing.at[r, h, :, cut], arrived.at[r, h, :, cut],
            scan_send.at[r, h], scan_recv.at[r, h], (lax.rem(seq + 2**r, NSEQ), fsdp),
        )

    def send_window(r, h):
        outgoing[r, h] = window[h].astype(BF16)

        @pl.when(seq + 2**r < NSEQ)
        def _():
            scan_copy(r, h).start()

    def chunks_of(h):
        every = range(NCH)
        solved, seen, maps = [], [], []
        for n in every:
            at = pl.ds(n * DH, DH)
            k = act[2 + h // 2, at, :]
            c = cols[n][:, h : h + 1]
            b = cols[n][:, 4 + h : 5 + h]
            right = jnp.concatenate([b * act[4 + h, at, :], (b * jnp.exp(c)) * k], axis=1)
            solved.append(nn(system[n * NH + h], right))
        for n in every:
            c = cols[n][:, h : h + 1]
            last = small[n][h : h + 1, DH - 1 : DH]
            maps.append(nn(key_t[n * 2 + h // 2], solved[n] * jnp.exp(last - c)))
            seen.append(nn(scores[n * NH + h], solved[n]))
        so_far = None
        for n in every:
            at = pl.ds(n * DH, DH)
            last = small[n][h : h + 1, DH - 1 : DH]
            transfer = jnp.exp(last) * eye - maps[n][:, DH:]
            query_eff = jnp.exp(cols[n][:, h : h + 1]) * act[h // 2, at, :] - seen[n][:, DH:]
            if n == 0:
                qt_ref[h, at, :] = query_eff.astype(BF16)
                core_ref[h, at, :] = seen[n][:, :DH]
                so_far = jnp.concatenate([transfer, maps[n][:, :DH]], axis=1)
            else:
                both = nn(query_eff, so_far)
                qt_ref[h, at, :] = both[:, :DH].astype(BF16)
                core_ref[h, at, :] = seen[n][:, :DH] + both[:, DH:]
                after = nn(transfer, so_far)
                so_far = jnp.concatenate(
                    [after[:, :DH], after[:, DH:] + maps[n][:, :DH]], axis=1
                )
        window[h] = so_far
        before[h] = jnp.zeros((DH, 2 * DH), F32)
        send_window(0, h)

    def compose(later, earlier):
        high, low = split(later[:, 0:DH])
        dot = functools.partial(jnp.dot, preferred_element_type=F32)
        return dot(high, earlier) + dot(low, earlier)

    def scan_step(r, h):
        step = 2**r

        @pl.when(seq >= step)
        def _():
            scan_copy(r, h).wait_recv()
            if r < ROUNDS - 1:
                out = compose(window[h], arrived[r, h])
                window[h, :, DH:] = out[:, DH:] + window[h, :, DH:]
                window[h, :, 0:DH] = out[:, :DH]

        if r < ROUNDS - 1:
            send_window(r + 1, h)

        @pl.when(seq >= step)
        def _():
            if r == 0:
                before[h] = arrived[r, h].astype(F32)
            elif r < ROUNDS - 1:
                out = compose(before[h], arrived[r, h])
                before[h, :, DH:] = out[:, DH:] + before[h, :, DH:]
                before[h, :, 0:DH] = out[:, :DH]
            else:
                out = compose(before[h], arrived[r, h, :, DH:])
                before[h, :, DH:] = out + before[h, :, DH:]

    mates = [sibling, across, cross]

    def gate_copy(i, h):
        rows = pl.ds(pl.multiple_of(mates[i][1] * TOK, TOK), TOK)
        return remote(
            gated.at[h, rows], gated_all.at[fsdp * NH + h],
            gate_send.at[i, h], gate_recv.at[i, h], mates[i],
        )

    def finish(h):
        core_rows = core_ref[h] + nn(qt_ref[h], before[h, :, DH:])
        scale = lax.rsqrt(jnp.mean(core_rows * core_rows, axis=-1, keepdims=True) + 1e-6)
        z = gate_ref[:, pl.ds(h * DH, DH)].astype(F32)
        gain = gain_ref[...].reshape(1, DH)
        gated[h] = (core_rows * scale * gain * silu(z)).astype(BF16)
        for i in (1, 2, 0):
            gate_copy(i, h).start()
        gated_all[fsdp * NH + h] = gated[h, pl.ds(pl.multiple_of(fsdp * TOK, TOK), TOK), :]

    for wave in range(NH + ROUNDS - 1):
        if wave < NH:
            chunks_of(wave)
        if wave == 1:
            wo_cut().wait_recv()
            for i in range(3):
                wo_round(i).start()
        if wave == NH:
            arrive(3)
            for j in range(2):
                gate_ref[:, pl.ds(j * 256, 256)] = project(4 + j)[HALO:].astype(BF16)
            for i in range(3):
                wo_round(i).wait_recv()
            wo_share().start()
        for h in range(NH):
            r = wave - 1 - h
            if 0 <= r < ROUNDS:
                scan_step(r, h)
                if r == ROUNDS - 1:
                    finish(h)
    scan_step(ROUNDS - 1, NH - 1)
    finish(NH - 1)

    def terms(groups, first):
        for j in range(D // 512):
            at = pl.ds(j * 512, 512)
            total = None if first else total_ref[:, at]
            for group in groups:
                held_rows = jnp.concatenate(
                    [gated_all[group * NH + h] for h in range(NH)], axis=1
                )
                term = jnp.dot(held_rows, wo_all[group, :, at], preferred_element_type=F32)
                total = term if total is None else total + term
            if first:
                total_ref[:, at] = total
            else:
                out_ref[:, at] = total.astype(BF16)

    local_copies[6].wait()
    wo_beside().wait_recv()
    for h in range(NH):
        gate_copy(0, h).wait_recv()
    terms((fsdp, sibling[1]), True)
    wo_share().wait_recv()
    for h in range(NH):
        for i in (1, 2):
            gate_copy(i, h).wait_recv()
    terms((far, far + 1), False)

    tok_copies[0].wait_send()
    tok_copies[1].wait_send()
    pass_on.wait_send()
    for copy in ba_copies + near_copies:
        copy.wait_send()
    for section in range(4):
        for i in range(2):
            cut_copy(section, i).wait_send()
        for shard in range(2):
            for i in range(3):
                ring_copy(section, shard, i).wait_send()

    @pl.when(sends_halo)
    def _():
        for k in range(4):
            halo_copy(k).wait_send()

    wo_beside().wait_send()
    wo_cut().wait_send()
    for i in range(3):
        wo_round(i).wait_send()
    wo_share().wait_send()
    for r in range(ROUNDS):
        @pl.when(seq + 2**r < NSEQ)
        def _():
            for h in range(NH):
                scan_copy(r, h).wait_send()
    for h in range(NH):
        for i in range(3):
            gate_copy(i, h).wait_send()


def layer(
    tokens, w_query, w_key, w_value, w_gate, wba, w_out, conv_weight, decay_log, dt_bias, norm_gain
):
    return pl.pallas_call(
        layer_kernel,
        out_shape=jax.ShapeDtypeStruct((TOK, D), BF16),
        in_specs=[HBM] * 5 + [VMEM, HBM, VMEM, SMEM, SMEM, VMEM],
        out_specs=VMEM,
        scratch_shapes=[
            pltpu.VMEM((ROWS, D), BF16),
            pltpu.VMEM((4, DSH, GC), BF16),
            pltpu.VMEM((4, 32, DSH), BF16),
            pltpu.VMEM((ROWS, 256), F32),
            pltpu.VMEM((8, BLK, DH), F32),
            pltpu.VMEM((NCH, 8, DH), F32),
            pltpu.VMEM((NCH, DH, 8), F32),
            pltpu.VMEM((NCH * 2, DH, DH), BF16),
            pltpu.VMEM((UNITS, DH, DH), BF16),
            pltpu.VMEM((UNITS, DH, DH), BF16),
            pltpu.VMEM((NH, BLK, DH), F32),
            pltpu.VMEM((NH, BLK, DH), BF16),
            pltpu.VMEM((BLK, GV), BF16),
            pltpu.VMEM((4, DSH, D), BF16),
            pltpu.VMEM((ROUNDS, NH, DH, 2 * DH), BF16),
            pltpu.VMEM((ROUNDS, NH, DH, 2 * DH), BF16),
            pltpu.VMEM((NH, DH, 2 * DH), F32),
            pltpu.VMEM((NH, DH, 2 * DH), F32),
            pltpu.VMEM((NH, BLK, DH), BF16),
            pltpu.VMEM((4 * NH, TOK, DH), BF16),
            pltpu.VMEM((TOK, D), F32),
            DMA((7,)), DMA((4,)), DMA((3,)), DMA((3,)), DMA((4,)), DMA((4,)),
            DMA((2, 4)), DMA((2, 4)), DMA((2, 3, 4)), DMA((2, 3, 4)), DMA((7,)),
            DMA((6,)), DMA((6,)), DMA((ROUNDS, NH)), DMA((ROUNDS, NH)), DMA((3, NH)), DMA((3, NH)),
        ],
        compiler_params=pltpu.CompilerParams(
            collective_id=0, has_side_effects=True, vmem_limit_bytes=54 << 20
        ),
        name="layer",
    )(
        tokens, w_query, w_key, w_value, w_gate, wba, w_out, conv_weight, decay_log, dt_bias, norm_gain
    )


def shards(
    tokens, w_query, w_key, w_value, w_gate_out, w_beta, w_decay,
    conv_weight, decay_log, dt_bias, norm_gain, w_out,
):
    wba = jnp.concatenate([w_beta, w_decay], axis=1).T
    return layer(
        tokens, w_query, w_key, w_value, w_gate_out, wba, w_out,
        conv_weight, decay_log, dt_bias, norm_gain,
    )


def solution(mesh):
    return jax.shard_map(
        shards,
        mesh=mesh,
        in_specs=(
            P(("seq", "fsdp"), None),
            P("fsdp", None), P("fsdp", None), P("fsdp", None), P("fsdp", None),
            P("fsdp", None), P("fsdp", None),
            P(), P(), P(), P(),
            P("fsdp", None),
        ),
        out_specs=P(("seq", "fsdp"), None),
        check_vma=False,
    )
```

time: 179 us -> 114 us (0.64)
  the two profiles are of different devices: /device:TPU:21 before, /device:TPU:47 now
where the time goes in v3:
time: 114 us
  Pallas kernels  110 us (96%)
  local copies, waits for them, and re-layouts  1.88 us (2%)
  other arithmetic  1.35 us (1%)
    pallas_call x1, Pallas kernels, layer(): pl.pallas_call(layer_kernel, out_shape=jax.ShapeDtypeStruct((TOK, D), BF1...  110 us

profile of v3, /device:TPU:47, one launch (start us, length us, event | category | flops | bytes accessed | tf_op | source)
XLA Modules:
  0.0 113.6 jit_solution(1070560516931166317)
XLA Ops:
  0.0 1.4 %maximum_bitcast_fusion.wba_ref = bf16[32,512]{1,0:T(8,128)(2,1)} fusion(bf16[512,16]{0,1:T(8,128)(2,1)} %param.18, bf16[512,16]{0,1:T(8,128)(2,1)} %param.17), kind=kLoop, calls=%fused_computation | loop fusion | flops 65536 | bytes 65536 | tf_op jit(solution)/shard_map/transpose | solution.py:606
  1.4 110.3 %layer.1 = bf16[128,2048]{1,0:T(8,128)(2,1)} custom-call(bf16[128,2048]{1,0:T(8,128)(2,1)} %tok_ref.1, bf16[512,1024]{1,0:T(8,128)(2,1)} %wq_ref.1, bf16[512,1024]{1,0:T(8,128)(2,1)} %wk_ref.1, bf16[512,2048]{1,0:T(8,128)(2,1)} %wv_ref.1, bf16[512,2048]{1,0:T(8,128)(2,1)} %wz_ref.1, bf16[32,512]{1,0:T(8,128)(2,1)} %maximum_bitcast_fusion.wba_ref, ...), custom_call_target="tpu_custom_call" | custom-call | tf_op jit(solution)/shard_map/layer/pallas_call | solution.py:562
  111.7 1.9 %copy.14 = bf16[128,2048]{1,0:T(8,128)(2,1)} copy(bf16[128,2048]{1,0:T(8,128)(2,1)} %layer.1) | data formatting | bytes 1048576

commit v4 on v3

--- a/solution.py
+++ b/solution.py
@@ -54,6 +54,8 @@
 
 SECTIONS = ((0, GQ), (GQ, GQ), (2 * GQ, GV), (2 * GQ + GV, GV))
 PIECE = DSH // 4
+HALF = PIECE // 2
+STAGES = ((0, 2 * GQ, (0, 1)), (2 * GQ, GV, (2,)), (2 * GQ + GV, GV, (3,)))
 UNITS = NCH * NH
 TOGETHER = 8
 
@@ -62,16 +64,17 @@
     tok_ref, wq_ref, wk_ref, wv_ref, wz_ref, wba_ref, wo_ref, conv_ref, rate_ref, bias_ref, gain_ref,
     out_ref,
     tok_all, w_all, wba_all, mixed, act, small, cols, key_t, system, scores,
-    core_ref, qt_ref, gate_ref, wo_all, outgoing, arrived, window, before, gated, gated_all, total_ref,
+    core_ref, qt_ref, gate_ref, wo_all, outgoing, arrived, window, before, gated, gated_far, total_ref,
+    sums_out, sums_in,
     tok_send, tok_recv, ba_send, ba_recv, near_send, near_recv, cut_send, cut_recv,
-    ring_send, ring_recv, loc, wo_send, wo_recv, scan_send, scan_recv, gate_send, gate_recv,
+    pair_send, pair_recv, ring_send, ring_recv, loc, wo_send, wo_recv, scan_send, scan_recv, gate_send, gate_recv,
+    sum_send, sum_recv,
 ):
     seq, fsdp, zlo, zhi, core = coords()
     x, y = seq // 8, (seq // 2) % 4
     sibling = (seq, zhi * 2 + 1 - core)
     far = (1 - zhi) * 2
     across = (seq, far + core)
-    cross = (seq, far + 1 - core)
     partner = seq - zlo + 1 - zlo
     partners = [(partner, far + core), (partner, far + 1 - core)]
     rings = [
@@ -80,8 +83,9 @@
     ]
     sends_halo = jnp.logical_and(fsdp == 3, seq < NSEQ - 1)
 
+    twin = (seq - zlo + 1 - zlo, fsdp)
     barrier = pltpu.get_barrier_semaphore()
-    for peer in [sibling, across, cross] + partners + rings[0] + rings[1]:
+    for peer in [sibling, across, twin] + partners + rings[0] + rings[1]:
         pl.semaphore_signal(barrier, inc=1, device_id=peer, device_id_type=MESH)
     for r in range(ROUNDS):
         @pl.when(seq >= 2**r)
@@ -116,7 +120,7 @@
     local = [(tok_ref, token_rows(fsdp)), (wba_ref, wba_all.at[fsdp])] + [
         (weights[section].at[:, columns(section, fsdp)], held(fsdp, all_rows, section))
         for section in range(4)
-    ] + [(wo_ref, wo_all.at[fsdp])]
+    ] + [(wo_ref, wo_all.at[0])]
     local_copies = [
         pltpu.make_async_copy(source, target, loc.at[i])
         for i, (source, target) in enumerate(local)
@@ -134,97 +138,113 @@
     for copy in tok_copies:
         copy.start()
 
+    def halo_copy(k):
+        return remote(
+            tok_ref.at[pl.ds(TOK - HALO, HALO)], tok_all.at[pl.ds(0, HALO)],
+            tok_send.at[3 + k], tok_recv.at[3], (lax.rem(seq + 1, NSEQ), k),
+        )
+
+    ba_copies = [
+        remote(wba_ref, wba_all.at[fsdp], ba_send.at[i], ba_recv.at[i], peer)
+        for i, peer in enumerate([sibling] + partners)
+    ]
+
     piece_at = jnp.where(core == 0, x, y)
-    own_piece = pl.ds(pl.multiple_of(piece_at * PIECE, PIECE), PIECE)
+    places = [x, y]
+
+    def half_rows(place, half):
+        return pl.ds(pl.multiple_of(place * PIECE + half * HALF, HALF), HALF)
 
     def cut_copy(section, i):
         peer = partners[i]
-        return remote(
-            weights[section].at[own_piece, columns(section, peer[1])],
-            held(fsdp, own_piece, section),
+        rows = half_rows(piece_at, 1 - zlo)
+        return remote(
+            weights[section].at[rows, columns(section, peer[1])],
+            held(fsdp, rows, section),
             cut_send.at[i, section], cut_recv.at[core, section], peer,
         )
 
-    for section in range(4):
-        for i in range(2):
-            cut_copy(section, i).start()
-
-    def halo_copy(k):
-        return remote(
-            tok_ref.at[pl.ds(TOK - HALO, HALO)], tok_all.at[pl.ds(0, HALO)],
-            tok_send.at[3 + k], tok_recv.at[3], (lax.rem(seq + 1, NSEQ), k),
-        )
+    def near_copy(section):
+        return remote(
+            weights[section].at[:, columns(section, sibling[1])],
+            held(fsdp, all_rows, section),
+            near_send.at[section], near_recv.at[section], sibling,
+        )
+
+    def start_stage(stage):
+        for section in STAGES[stage][2]:
+            for i in range(2):
+                cut_copy(section, i).start()
+            near_copy(section).start()
+
+    def block_of(stage, shard, half):
+        start, width, _ = STAGES[stage]
+        return w_all.at[far + shard, half_rows(places[shard], half), pl.ds(start, width)]
+
+    def pair_copy(stage, shard):
+        block = block_of(stage, shard, zlo)
+        return remote(
+            block, block, pair_send.at[shard, stage], pair_recv.at[shard, stage], twin
+        )
+
+    def ring_copy(stage, shard, which, i):
+        block = block_of(stage, shard, zlo if which == 0 else 1 - zlo)
+        return remote(
+            block, block, ring_send.at[stage, which, shard, i],
+            ring_recv.at[stage, which, shard, i], rings[shard][i],
+        )
+
+    def pass_cut(stage):
+        for shard in range(2):
+            for section in STAGES[stage][2]:
+                block = held(far + shard, half_rows(places[shard], zlo), section)
+                remote(
+                    block, block, cut_send.at[0, section], cut_recv.at[shard, section],
+                    partners[0],
+                ).wait_recv()
+            pair_copy(stage, shard).start()
+            for i in range(3):
+                ring_copy(stage, shard, 0, i).start()
+
+    def pass_pair(stage):
+        for shard in range(2):
+            pair_copy(stage, shard).wait_recv()
+            for i in range(3):
+                ring_copy(stage, shard, 1, i).start()
+
+    def arrive(stage):
+        for section in STAGES[stage][2]:
+            local_copies[2 + section].wait()
+            near_copy(section).wait_recv()
+        for which in range(2):
+            for shard in range(2):
+                for i in range(3):
+                    ring_copy(stage, shard, which, i).wait_recv()
+
+    wo_at = pl.ds(pl.multiple_of(piece_at * PIECE, PIECE), PIECE)
+    wo_ring = [
+        (jnp.where(core == 0, rings[0][i][0], rings[1][i][0]), fsdp) for i in range(3)
+    ]
+
+    def wo_cut():
+        return remote(
+            wo_ref.at[wo_at], wo_all.at[1, wo_at], wo_send.at[0], wo_recv.at[0], partners[0]
+        )
+
+    def wo_round(i):
+        block = wo_all.at[1, wo_at]
+        return remote(block, block, wo_send.at[1 + i], wo_recv.at[1 + i], wo_ring[i])
+
+    start_stage(0)
 
     @pl.when(sends_halo)
     def _():
         for k in range(4):
             halo_copy(k).start()
 
-    ba_copies = [
-        remote(wba_ref, wba_all.at[fsdp], ba_send.at[i], ba_recv.at[i], peer)
-        for i, peer in enumerate([sibling] + partners)
-    ]
     for copy in ba_copies:
         copy.start()
-
-    near_copies = [
-        remote(
-            weights[section].at[:, columns(section, sibling[1])],
-            held(fsdp, all_rows, section),
-            near_send.at[section], near_recv.at[section], sibling,
-        )
-        for section in range(4)
-    ]
-    for copy in near_copies:
-        copy.start()
-
-    places = [x, y]
-
-    def ring_copy(section, shard, i):
-        rows = pl.ds(pl.multiple_of(places[shard] * PIECE, PIECE), PIECE)
-        block = held(far + shard, rows, section)
-        return remote(
-            block, block, ring_send.at[shard, i, section], ring_recv.at[shard, i, section],
-            rings[shard][i],
-        )
-
-    def pass_round(section):
-        for shard in range(2):
-            rows = pl.ds(pl.multiple_of(places[shard] * PIECE, PIECE), PIECE)
-            block = held(far + shard, rows, section)
-            remote(
-                block, block, cut_send.at[0, section], cut_recv.at[shard, section], partners[0]
-            ).wait_recv()
-            for i in range(3):
-                ring_copy(section, shard, i).start()
-
-    wo_at = pl.ds(pl.multiple_of(piece_at * PIECE, PIECE), PIECE)
-    wo_ring = [
-        (jnp.where(core == 0, rings[0][i][0], rings[1][i][0]), fsdp) for i in range(3)
-    ]
-
-    def wo_beside():
-        return remote(wo_ref, wo_all.at[fsdp], wo_send.at[0], wo_recv.at[0], sibling)
-
-    def wo_cut():
-        return remote(
-            wo_ref.at[wo_at], wo_all.at[fsdp, wo_at], wo_send.at[1], wo_recv.at[1], partners[0]
-        )
-
-    def wo_round(i):
-        block = wo_all.at[far + core, wo_at]
-        return remote(block, block, wo_send.at[2 + i], wo_recv.at[2 + i], wo_ring[i])
-
-    def wo_share():
-        block = wo_all.at[far + core]
-        return remote(block, block, wo_send.at[5], wo_recv.at[5], sibling)
-
-    def arrive(section):
-        local_copies[2 + section].wait()
-        near_copies[section].wait_recv()
-        for shard in range(2):
-            for i in range(3):
-                ring_copy(section, shard, i).wait_recv()
+    start_stage(1)
 
     def project(j):
         total = None
@@ -268,13 +288,16 @@
     eye = (at_row == at_col).astype(F32)
     upper = (at_row <= at_col).astype(F32)
 
-    pass_round(0)
+    pass_cut(0)
+    pass_pair(0)
     tok_copies[0].wait_recv()
     pass_on = remote(
         token_rows(across[1]), token_rows(across[1]), tok_send.at[2], tok_recv.at[2], sibling
     )
     pass_on.start()
-    pass_round(1)
+    pass_cut(1)
+    start_stage(2)
+    pass_pair(1)
 
     local_copies[0].wait()
     local_copies[1].wait()
@@ -316,10 +339,7 @@
 
     arrive(0)
     convolve(0)
-    pass_round(2)
-    arrive(1)
     convolve(1)
-    pass_round(3)
 
     def fall_of(n, h):
         gap = cols[n][:, h : h + 1] - small[n][h : h + 1, :]
@@ -341,6 +361,7 @@
         return carry
 
     lax.fori_loop(0, NCH, pairs, 0)
+    pass_cut(2)
 
     def same(size):
         return at_row // size == at_col // size
@@ -368,25 +389,33 @@
 
     lax.fori_loop(0, UNITS // TOGETHER, invert, 0)
 
-    arrive(2)
-    wo_beside().start()
+    pass_pair(2)
     wo_cut().start()
+    arrive(1)
     convolve(2)
     convolve(3)
 
-    def scan_copy(r, h):
-        cut = pl.ds(0, 2 * DH) if r < ROUNDS - 1 else pl.ds(DH, DH)
+    def scan_copy(r, h, part):
+        cut = pl.ds(part * DH, DH)
         return remote(
             outgoing.at[r, h, :, cut], arrived.at[r, h, :, cut],
-            scan_send.at[r, h], scan_recv.at[r, h], (lax.rem(seq + 2**r, NSEQ), fsdp),
-        )
-
-    def send_window(r, h):
-        outgoing[r, h] = window[h].astype(BF16)
+            scan_send.at[r, h, part], scan_recv.at[r, h, part],
+            (lax.rem(seq + 2**r, NSEQ), fsdp),
+        )
+
+    def parts(r):
+        return (0, 1) if r < ROUNDS - 1 else (1,)
+
+    def send_part(r, h, part, value):
+        outgoing[r, h, :, pl.ds(part * DH, DH)] = value.astype(BF16)
 
         @pl.when(seq + 2**r < NSEQ)
         def _():
-            scan_copy(r, h).start()
+            scan_copy(r, h, part).start()
+
+    def send_window(r, h):
+        for part in parts(r):
+            send_part(r, h, part, window[h, :, pl.ds(part * DH, DH)])
 
     def chunks_of(h):
         every = range(NCH)
@@ -426,7 +455,7 @@
         send_window(0, h)
 
     def compose(later, earlier):
-        high, low = split(later[:, 0:DH])
+        high, low = later
         dot = functools.partial(jnp.dot, preferred_element_type=F32)
         return dot(high, earlier) + dot(low, earlier)
 
@@ -435,34 +464,39 @@
 
         @pl.when(seq >= step)
         def _():
-            scan_copy(r, h).wait_recv()
             if r < ROUNDS - 1:
-                out = compose(window[h], arrived[r, h])
-                window[h, :, DH:] = out[:, DH:] + window[h, :, DH:]
-                window[h, :, 0:DH] = out[:, :DH]
+                own = split(window[h, :, 0:DH])
+                scan_copy(r, h, 0).wait_recv()
+                if r < ROUNDS - 2:
+                    moved = compose(own, arrived[r, h, :, 0:DH])
+                    send_part(r + 1, h, 0, moved)
+                    window[h, :, 0:DH] = moved
+                scan_copy(r, h, 1).wait_recv()
+                shifted = compose(own, arrived[r, h, :, DH:]) + window[h, :, DH:]
+                send_part(r + 1, h, 1, shifted)
+                window[h, :, DH:] = shifted
+                if r == 0:
+                    before[h] = arrived[r, h].astype(F32)
+                else:
+                    out = compose(split(before[h, :, 0:DH]), arrived[r, h])
+                    before[h, :, DH:] = out[:, DH:] + before[h, :, DH:]
+                    before[h, :, 0:DH] = out[:, :DH]
+            else:
+                own = split(before[h, :, 0:DH])
+                scan_copy(r, h, 1).wait_recv()
+                before[h, :, DH:] = compose(own, arrived[r, h, :, DH:]) + before[h, :, DH:]
 
         if r < ROUNDS - 1:
-            send_window(r + 1, h)
-
-        @pl.when(seq >= step)
-        def _():
-            if r == 0:
-                before[h] = arrived[r, h].astype(F32)
-            elif r < ROUNDS - 1:
-                out = compose(before[h], arrived[r, h])
-                before[h, :, DH:] = out[:, DH:] + before[h, :, DH:]
-                before[h, :, 0:DH] = out[:, :DH]
-            else:
-                out = compose(before[h], arrived[r, h, :, DH:])
-                before[h, :, DH:] = out + before[h, :, DH:]
-
-    mates = [sibling, across, cross]
-
-    def gate_copy(i, h):
-        rows = pl.ds(pl.multiple_of(mates[i][1] * TOK, TOK), TOK)
-        return remote(
-            gated.at[h, rows], gated_all.at[fsdp * NH + h],
-            gate_send.at[i, h], gate_recv.at[i, h], mates[i],
+            @pl.when(seq < step)
+            def _():
+                send_window(r + 1, h)
+
+    here = pl.ds(pl.multiple_of(zhi * 2 * TOK, TOK), 2 * TOK)
+    there = pl.ds(pl.multiple_of(far * TOK, TOK), 2 * TOK)
+
+    def gate_copy(h):
+        return remote(
+            gated.at[h, there], gated_far.at[h], gate_send.at[h], gate_recv.at[h], across
         )
 
     def finish(h):
@@ -471,24 +505,19 @@
         z = gate_ref[:, pl.ds(h * DH, DH)].astype(F32)
         gain = gain_ref[...].reshape(1, DH)
         gated[h] = (core_rows * scale * gain * silu(z)).astype(BF16)
-        for i in (1, 2, 0):
-            gate_copy(i, h).start()
-        gated_all[fsdp * NH + h] = gated[h, pl.ds(pl.multiple_of(fsdp * TOK, TOK), TOK), :]
+        gate_copy(h).start()
 
     for wave in range(NH + ROUNDS - 1):
         if wave < NH:
             chunks_of(wave)
-        if wave == 1:
+        if wave == 3:
             wo_cut().wait_recv()
             for i in range(3):
                 wo_round(i).start()
-        if wave == NH:
-            arrive(3)
+        if wave == 5:
+            arrive(2)
             for j in range(2):
                 gate_ref[:, pl.ds(j * 256, 256)] = project(4 + j)[HALO:].astype(BF16)
-            for i in range(3):
-                wo_round(i).wait_recv()
-            wo_share().start()
         for h in range(NH):
             r = wave - 1 - h
             if 0 <= r < ROUNDS:
@@ -498,62 +527,69 @@
     scan_step(ROUNDS - 1, NH - 1)
     finish(NH - 1)
 
-    def terms(groups, first):
-        for j in range(D // 512):
-            at = pl.ds(j * 512, 512)
-            total = None if first else total_ref[:, at]
-            for group in groups:
-                held_rows = jnp.concatenate(
-                    [gated_all[group * NH + h] for h in range(NH)], axis=1
-                )
-                term = jnp.dot(held_rows, wo_all[group, :, at], preferred_element_type=F32)
-                total = term if total is None else total + term
-            if first:
-                total_ref[:, at] = total
-            else:
-                out_ref[:, at] = total.astype(BF16)
+    mine = pl.ds(pl.multiple_of(core * TOK, TOK), TOK)
+    others = pl.ds(pl.multiple_of((1 - core) * TOK, TOK), TOK)
+
+    def sum_copy(j):
+        at = pl.ds(j * 512, 512)
+        return remote(
+            sums_out.at[:, at], sums_in.at[:, at], sum_send.at[j], sum_recv.at[j], sibling
+        )
 
     local_copies[6].wait()
-    wo_beside().wait_recv()
+    own_rows = jnp.concatenate([gated[h, here, :] for h in range(NH)], axis=1)
+    for j in range(D // 512):
+        at = pl.ds(j * 512, 512)
+        total_ref[:, at] = jnp.dot(own_rows, wo_all[0, :, at], preferred_element_type=F32)
+    for i in range(3):
+        wo_round(i).wait_recv()
     for h in range(NH):
-        gate_copy(0, h).wait_recv()
-    terms((fsdp, sibling[1]), True)
-    wo_share().wait_recv()
-    for h in range(NH):
-        for i in (1, 2):
-            gate_copy(i, h).wait_recv()
-    terms((far, far + 1), False)
+        gate_copy(h).wait_recv()
+    far_rows = jnp.concatenate([gated_far[h] for h in range(NH)], axis=1)
+    for j in range(D // 512):
+        at = pl.ds(j * 512, 512)
+        total_ref[:, at] += jnp.dot(far_rows, wo_all[1, :, at], preferred_element_type=F32)
+        sums_out[:, at] = total_ref[others, at].astype(BF16)
+        sum_copy(j).start()
+    for j in range(D // 512):
+        at = pl.ds(j * 512, 512)
+        sum_copy(j).wait_recv()
+        out_ref[:, at] = (total_ref[mine, at] + sums_in[:, at].astype(F32)).astype(BF16)
 
     tok_copies[0].wait_send()
     tok_copies[1].wait_send()
     pass_on.wait_send()
-    for copy in ba_copies + near_copies:
+    for copy in ba_copies:
         copy.wait_send()
     for section in range(4):
+        near_copy(section).wait_send()
         for i in range(2):
             cut_copy(section, i).wait_send()
+    for stage in range(3):
         for shard in range(2):
-            for i in range(3):
-                ring_copy(section, shard, i).wait_send()
+            pair_copy(stage, shard).wait_send()
+            for which in range(2):
+                for i in range(3):
+                    ring_copy(stage, shard, which, i).wait_send()
 
     @pl.when(sends_halo)
     def _():
         for k in range(4):
             halo_copy(k).wait_send()
 
-    wo_beside().wait_send()
     wo_cut().wait_send()
     for i in range(3):
         wo_round(i).wait_send()
-    wo_share().wait_send()
     for r in range(ROUNDS):
         @pl.when(seq + 2**r < NSEQ)
         def _():
             for h in range(NH):
-                scan_copy(r, h).wait_send()
+                for part in parts(r):
+                    scan_copy(r, h, part).wait_send()
     for h in range(NH):
-        for i in range(3):
-            gate_copy(i, h).wait_send()
+        gate_copy(h).wait_send()
+    for j in range(D // 512):
+        sum_copy(j).wait_send()
 
 
 def layer(
@@ -578,17 +614,21 @@
             pltpu.VMEM((NH, BLK, DH), F32),
             pltpu.VMEM((NH, BLK, DH), BF16),
             pltpu.VMEM((BLK, GV), BF16),
-            pltpu.VMEM((4, DSH, D), BF16),
+            pltpu.VMEM((2, DSH, D), BF16),
             pltpu.VMEM((ROUNDS, NH, DH, 2 * DH), BF16),
             pltpu.VMEM((ROUNDS, NH, DH, 2 * DH), BF16),
             pltpu.VMEM((NH, DH, 2 * DH), F32),
             pltpu.VMEM((NH, DH, 2 * DH), F32),
             pltpu.VMEM((NH, BLK, DH), BF16),
-            pltpu.VMEM((4 * NH, TOK, DH), BF16),
-            pltpu.VMEM((TOK, D), F32),
+            pltpu.VMEM((NH, 2 * TOK, DH), BF16),
+            pltpu.VMEM((2 * TOK, D), F32),
+            pltpu.VMEM((TOK, D), BF16),
+            pltpu.VMEM((TOK, D), BF16),
             DMA((7,)), DMA((4,)), DMA((3,)), DMA((3,)), DMA((4,)), DMA((4,)),
-            DMA((2, 4)), DMA((2, 4)), DMA((2, 3, 4)), DMA((2, 3, 4)), DMA((7,)),
-            DMA((6,)), DMA((6,)), DMA((ROUNDS, NH)), DMA((ROUNDS, NH)), DMA((3, NH)), DMA((3, NH)),
+            DMA((2, 4)), DMA((2, 4)), DMA((2, 3)), DMA((2, 3)),
+            DMA((3, 2, 2, 3)), DMA((3, 2, 2, 3)), DMA((7,)),
+            DMA((4,)), DMA((4,)), DMA((ROUNDS, NH, 2)), DMA((ROUNDS, NH, 2)), DMA((NH,)), DMA((NH,)),
+            DMA((4,)), DMA((4,)),
         ],
         compiler_params=pltpu.CompilerParams(
             collective_id=0, has_side_effects=True, vmem_limit_bytes=54 << 20

time: 114 us -> 104 us (0.912)
  the two profiles are of different devices: /device:TPU:47 before, /device:TPU:103 now
where the time goes in v4:
time: 104 us
  Pallas kernels  100 us (96%)
  local copies, waits for them, and re-layouts  1.88 us (2%)
  other arithmetic  1.35 us (1%)
    pallas_call x1, Pallas kernels, layer(): pl.pallas_call(layer_kernel, out_shape=jax.ShapeDtypeStruct((TOK, D), BF1...  100 us

profile of v4, /device:TPU:103, one launch (start us, length us, event | category | flops | bytes accessed | tf_op | source)
XLA Modules:
  0.0 103.6 jit_solution(16963023182895859246)
XLA Ops:
  0.0 1.4 %maximum_bitcast_fusion.wba_ref = bf16[32,512]{1,0:T(8,128)(2,1)} fusion(bf16[512,16]{0,1:T(8,128)(2,1)} %param.18, bf16[512,16]{0,1:T(8,128)(2,1)} %param.17), kind=kLoop, calls=%fused_computation | loop fusion | flops 65536 | bytes 65536 | tf_op jit(solution)/shard_map/transpose | solution.py:646
  1.4 100.3 %layer.1 = bf16[128,2048]{1,0:T(8,128)(2,1)} custom-call(bf16[128,2048]{1,0:T(8,128)(2,1)} %tok_ref.1, bf16[512,1024]{1,0:T(8,128)(2,1)} %wq_ref.1, bf16[512,1024]{1,0:T(8,128)(2,1)} %wk_ref.1, bf16[512,2048]{1,0:T(8,128)(2,1)} %wv_ref.1, bf16[512,2048]{1,0:T(8,128)(2,1)} %wz_ref.1, bf16[32,512]{1,0:T(8,128)(2,1)} %maximum_bitcast_fusion.wba_ref, ...), custom_call_target="tpu_custom_call" | custom-call | tf_op jit(solution)/shard_map/layer/pallas_call | solution.py:598
  101.7 1.9 %copy.14 = bf16[128,2048]{1,0:T(8,128)(2,1)} copy(bf16[128,2048]{1,0:T(8,128)(2,1)} %layer.1) | data formatting | bytes 1048576
